TPU v7x, 512 devices: a whole 4x4x16 slice. The times are simulated.
512 devices in a mesh: blk: 32 (over x, z_lo), expert: 16 (over z_hi, y, core).
Axes of the slice: x: 4, y: 4, z: 16 (z_hi: 2, z_lo: 8; z = z_hi * 8 + z_lo), core: 2. Of those that a mesh axis runs over, the one named last changes fastest.
Arguments:
- short_draft: bfloat16 [1024, 64, 3, 512], P(('blk', 'expert')), may hold values from -42 to 42
- short_mask: int32 [1024, 64, 64], P(('blk', 'expert')), may hold values from 0 to 1, as said below
- short_keys: bfloat16 [1024, 128, 512], P(('blk', 'expert')), may hold values from -16 to 16
- short_values: bfloat16 [1024, 128, 512], P(('blk', 'expert')), may hold values from -6 to 6
- short_length: int32 [1024], P(('blk', 'expert')), may hold values from 1 to 128, 65536 in all
- short_x: bfloat16 [65536, 1024], P(('blk', 'expert')), may hold values from -44 to 44
- accepted: int32 [1024, 8], P(('blk', 'expert')), may hold values from 0 to 63, as said below
- long_draft: bfloat16 [32, 64, 3, 512], P('expert'), may hold values from -42 to 42
- long_mask: int32 [32, 64, 64], P('expert'), may hold values from 0 to 1, as said below
- long_keys: bfloat16 [32, 8192, 512], P('expert', 'blk'), may hold values from -15 to 15
- long_values: bfloat16 [32, 8192, 512], P('expert', 'blk'), may hold values from -6 to 6
- long_x: bfloat16 [32, 64, 1024], P('expert', 'blk'), may hold values from -44 to 44
- out_weight: bfloat16 [512, 1024], P('expert'), may hold values from -0.25 to 0.25
- norm_gain: bfloat16 [1024], replicated, may hold values from 0.099609375 to 1.8984375
- router: bfloat16 [1024, 16], replicated, may hold values from -0.1875 to 0.1875
- route_ids: int32 [67584, 2], P(('blk', 'expert')), may hold values from 0 to 15, all different within a row; in each aligned block of 132 rows (0 to 131, 132 to 263, ...) at most 21 rows name the same one
- expert_in: bfloat16 [16, 1408, 2, 1024], P('expert', 'blk'), may hold values from -0.1875 to 0.1875
- expert_out: bfloat16 [16, 1408, 1024], P('expert', 'blk'), may hold values from -0.15625 to 0.15625
Outputs:
- short_out: bfloat16 [65536, 1024], P(('blk', 'expert'))
- accepted_out: bfloat16 [1024, 8, 1024], P(('blk', 'expert'))
- long_out: bfloat16 [32, 64, 1024], P('expert', 'blk')
Inputs may be any that keep to these rules, and one draw needn't show every extreme that they name: short_mask[r, i, j] is 1 exactly when tree node j is node i or one of its ancestors; every node but the root 0 has a parent of smaller index. long_mask[r, i, j] is 1 exactly when tree node j is node i or one of its ancestors; every node but the root 0 has a parent of smaller index. accepted[r] lists 8 nodes of request r's tree, the root first and node 63 last, each the parent of the next. `route_ids`: a row's two experts differ; among the rows of one device no expert is named more than 21 times.
All inputs are finite; a program needn't handle non-finite values. No bound on the sum of `short_length` on one device may be relied on, other than what follows from the above.
Results may differ from a plain program's by a relative error of at most 0.011.
Values may be sent and summed in bfloat16 or wider, within the bound.
A program may use at most 64 MiB of HBM per device.

v0:
```python
import jax
import jax.numpy as jnp
from jax import lax
from jax.sharding import PartitionSpec as P

HEADS = 8
HD = 64


def combined_all(part, axis, combine):
    gathered = jax.tree.map(lambda a: lax.all_gather(a, axis), part)

    def take(source):
        return jax.tree.map(lambda a: lax.dynamic_index_in_dim(a, source, 0, False), gathered)

    return lax.fori_loop(
        1, lax.axis_size(axis), lambda source, state: combine(state, take(source)), take(0)
    )


def heads_of(tensor):
    return tensor.reshape(tensor.shape[:-1] + (HEADS, HD))


def block_part(queries, keyside, values, allowed):
    head_size = queries.shape[-1]
    scores = jnp.einsum(
        "rqhe,rkhe->rqhk", queries, keyside, preferred_element_type=jnp.float32
    ) * head_size ** (-0.5)
    scores = jnp.where(allowed[:, :, None, :], scores, -jnp.inf)
    peaks = jnp.max(scores, axis=-1)
    weights = jnp.exp(scores - peaks[..., None]).astype(jnp.bfloat16)
    totals = jnp.sum(weights.astype(jnp.float32), axis=-1)
    output = jnp.einsum("rqhk,rkhe->rqhe", weights, values, preferred_element_type=jnp.float32)
    return (peaks, totals, output.reshape(output.shape[0], output.shape[1], -1))


def expand(factor, output):
    shaped = output.reshape(factor.shape + (-1,))
    return (shaped * factor[..., None]).reshape(output.shape)


def divide(output, totals):
    shaped = output.reshape(totals.shape + (-1,))
    return (shaped / totals[..., None]).reshape(output.shape)


def pair_join(former, latter):
    highest = jnp.maximum(former[0], latter[0])
    former_scale = jnp.exp(former[0] - highest)
    latter_scale = jnp.exp(latter[0] - highest)
    totals = former_scale * former[1] + latter_scale * latter[1]
    output = expand(former_scale, former[2]) + expand(latter_scale, latter[2])
    return (highest, totals, output)


def finish(joined):
    return divide(joined[2], joined[1]).astype(jnp.bfloat16)


def on_device(
    short_draft,
    short_mask,
    short_keys,
    short_values,
    short_length,
    short_x,
    accepted,
    long_draft,
    long_mask,
    long_keys,
    long_values,
    long_x,
    out_weight,
    norm_gain,
    router,
    route_ids,
    expert_in,
    expert_out,
):
    short_count = short_draft.shape[0]
    tree_size = short_draft.shape[1]
    cache_size = short_keys.shape[1]
    model_width = out_weight.shape[1]
    short_queries = heads_of(short_draft[:, :, 0])
    visible = jnp.broadcast_to(
        jnp.arange(cache_size)[None, None, :] < short_length[:, None, None],
        (short_count, tree_size, cache_size),
    )
    short_cache = block_part(short_queries, heads_of(short_keys), heads_of(short_values), visible)
    short_tree = block_part(
        short_queries,
        heads_of(short_draft[:, :, 1]),
        heads_of(short_draft[:, :, 2]),
        short_mask == 1,
    )
    short_attn = finish(pair_join(short_cache, short_tree))
    long_count = long_keys.shape[0]
    cache_local = long_keys.shape[1]
    long_queries = heads_of(long_draft[:, :, 0])
    everything = jnp.ones((long_count, tree_size, cache_local), dtype=bool)
    local_part = block_part(long_queries, heads_of(long_keys), heads_of(long_values), everything)
    share_rows = tree_size // lax.axis_size("blk")
    share_start = lax.axis_index("blk") * share_rows
    merged = combined_all(local_part, "blk", pair_join)
    cache_part = tuple(
        (lax.dynamic_slice_in_dim(member, share_start, share_rows, 1) for member in merged)
    )
    share_queries = lax.dynamic_slice_in_dim(long_queries, share_start, share_rows, 1)
    share_mask = lax.dynamic_slice_in_dim(long_mask, share_start, share_rows, 1)
    long_tree = block_part(
        share_queries, heads_of(long_draft[:, :, 1]), heads_of(long_draft[:, :, 2]), share_mask == 1
    )
    long_attn = finish(pair_join(cache_part, long_tree))
    attn_rows = jnp.concatenate(
        [short_attn.reshape(-1, short_attn.shape[-1]), long_attn.reshape(-1, long_attn.shape[-1])],
        axis=0,
    )
    residual = jnp.concatenate([short_x, long_x.reshape(-1, model_width)], axis=0)
    row_count = attn_rows.shape[0]
    projected = jnp.dot(
        attn_rows,
        lax.all_gather(out_weight, "expert", axis=0, tiled=True),
        preferred_element_type=jnp.float32,
    )
    layer_state = (residual.astype(jnp.float32) + projected).astype(jnp.bfloat16)
    state_wide = layer_state.astype(jnp.float32)
    normed = (
        state_wide
        * lax.rsqrt(jnp.mean(state_wide * state_wide, axis=-1, keepdims=True) + 1e-06)
        * norm_gain.astype(jnp.float32)
    ).astype(jnp.bfloat16)
    gate_probs = jax.nn.sigmoid(jnp.dot(normed, router, preferred_element_type=jnp.float32))
    expert_count = router.shape[1]
    capacity = (row_count * 10 + 4 * expert_count - 1) // (4 * expert_count)
    one_hot = route_ids[:, :, None] == jnp.arange(expert_count, dtype=jnp.int32)[None, None, :]
    gate_pick = jnp.sum(jnp.where(one_hot, gate_probs[:, None, :], 0.0), axis=-1)
    flat_hot = one_hot.reshape(2 * row_count, expert_count).astype(jnp.int32)
    earlier = jnp.cumsum(flat_hot, axis=0) - flat_hot
    slot_in = jnp.sum(earlier * flat_hot, axis=-1)
    target = route_ids.reshape(-1) * capacity + slot_in
    placement = (
        jnp.arange(expert_count * capacity, dtype=jnp.int32)[:, None] == target[None, :]
    ).astype(jnp.bfloat16)
    dispatch = jnp.dot(
        placement, jnp.repeat(normed, 2, axis=0), preferred_element_type=jnp.float32
    ).astype(jnp.bfloat16)
    dispatch = dispatch.reshape(expert_count, capacity, model_width)
    received = lax.all_to_all(dispatch, "expert", split_axis=0, concat_axis=0, tiled=True)
    flat_rows = received.reshape(-1, model_width)
    weight_in = lax.all_gather(expert_in, "blk", axis=1, tiled=True)[0]
    weight_out = lax.all_gather(expert_out, "blk", axis=1, tiled=True)[0]
    gate_part = jnp.einsum(
        "rd,nd->rn", flat_rows, weight_in[:, 0, :], preferred_element_type=jnp.float32
    )
    up_part = jnp.einsum(
        "rd,nd->rn", flat_rows, weight_in[:, 1, :], preferred_element_type=jnp.float32
    )
    inner_act = (jax.nn.gelu(gate_part, approximate=True) * up_part).astype(jnp.bfloat16)
    expert_sum = jnp.dot(inner_act, weight_out, preferred_element_type=jnp.float32)
    expert_y = expert_sum.astype(jnp.bfloat16).reshape(expert_count, capacity, model_width)
    returned = lax.all_to_all(expert_y, "expert", split_axis=0, concat_axis=0, tiled=True)
    per_route = jnp.einsum(
        "sa,sd->ad",
        placement,
        returned.reshape(-1, model_width),
        preferred_element_type=jnp.float32,
    )
    moe_sum = jnp.sum(per_route.reshape(row_count, 2, model_width) * gate_pick[:, :, None], axis=1)
    layer_out = (state_wide + moe_sum).astype(jnp.bfloat16)
    short_total = short_x.shape[0]
    short_out = layer_out[:short_total]
    long_out = layer_out[short_total:].reshape(long_x.shape)
    accepted_out = jnp.take_along_axis(
        short_out.reshape(short_count, tree_size, model_width), accepted[:, :, None], axis=1
    )
    return (short_out, accepted_out, long_out)


def solution(mesh):
    return jax.shard_map(
        on_device,
        mesh=mesh,
        in_specs=(
            P(("blk", "expert"), None, None, None),
            P(("blk", "expert"), None, None),
            P(("blk", "expert"), None, None),
            P(("blk", "expert"), None, None),
            P(("blk", "expert")),
            P(("blk", "expert"), None),
            P(("blk", "expert"), None),
            P("expert", None, None, None),
            P("expert", None, None),
            P("expert", "blk", None),
            P("expert", "blk", None),
            P("expert", "blk", None),
            P("expert", None),
            P(),
            P(),
            P(("blk", "expert"), None),
            P("expert", "blk", None, None),
            P("expert", "blk", None),
        ),
        out_specs=(
            P(("blk", "expert"), None),
            P(("blk", "expert"), None, None),
            P("expert", "blk", None),
        ),
        check_vma=False,
    )
```

profile of v0, /device:TPU:1, one launch (start us, length us, event | category | flops | bytes accessed | tf_op | source)
XLA Modules:
  0.0 905.2 jit_solution(18083236764553195508)
XLA Ops:
  7.2 1.1 fusion.65
  8.5 1.2 copy.132
  11.1 0.9 all_gather_reshape.3
  12.0 0.7 all-gather.9.cloned.1.call-update
  12.8 0.7 all-gather.11.cloned.1.call-update
  13.5 0.8 copy.147
  14.3 0.4 convert_reduce_fusion
  14.8 119.0 %all-gather = f32[64,64,8]{1,2,0:T(8,128)S(1)} all-gather(f32[2,64,8]{1,2,0:T(8,128)S(1)} %get-tuple-element.216), channel_id=2, replica_groups=mesh['blk'=32,'expert'=16] {'blk'}, dimensions={0}, use_global_device_ids=true | all-gather | bytes 135168 | tf_op jit(solution)/shard_map/all_gather | solution.py:11
  133.8 103.8 %all-gather.1 = f32[64,64,8]{1,2,0:T(8,128)S(1)} all-gather(f32[2,64,8]{1,2,0:T(8,128)S(1)} %convert_reduce_fusion), channel_id=3, replica_groups=mesh['blk'=32,'expert'=16] {'blk'}, dimensions={0}, use_global_device_ids=true | all-gather | bytes 135168 | tf_op jit(solution)/shard_map/all_gather | solution.py:11
  240.0 0.4 convert_reduce_fusion.2
  240.8 0.5 fusion.30
  242.0 0.9 reduce-window.6
  243.2 0.7 dynamic-slice_compare_fusion
  244.4 9.7 %all-gather.7.cloned.1.call-done = f32[32,2,64,512]{3,2,1,0:T(8,128)} async-done(((f32[1,2,64,512]{3,2,1,0:T(8,128)}), f32[32,2,64,512]{3,2,1,0:T(8,128)}) %all-gather.7.cloned.1.call-update) | async-done | bytes 8388624 | tf_op jit(solution)/shard_map/all_gather | solution.py:11
  254.1 1.0 slice_bitcast_fusion.10
  255.1 62.8 %while.19 = (s32[]{:T(128)}, f32[2,64,8]{1,2,0:T(8,128)S(1)}, f32[2,64,8]{1,2,0:T(8,128)S(1)}, f32[2,64,512]{2,1,0:T(8,128)S(1)}, f32[32,2,64,8]{2,3,1,0:T(8,128...) while((s32[]{:T(128)}, f32[2,64,8]{1,2,0:T(8,128)S(1)}, ...), condition=%wide.region_7.8_spmd, body=%wide.region_6.7_spmd.sunk | while | flops 202757 | bytes 2941079 | solution.py:16
  256.0 1.1 fusion.84
  258.0 1.1 fusion.84
  260.1 1.1 fusion.84
  262.1 1.1 fusion.84
  264.1 1.1 fusion.84
  266.1 1.1 fusion.84
  268.2 1.1 fusion.84
  270.2 1.1 fusion.84
  272.2 1.1 fusion.84
  274.2 1.1 fusion.84
  276.3 1.1 fusion.84
  278.3 1.1 fusion.84
  280.3 1.1 fusion.84
  282.3 1.1 fusion.84
  284.4 1.1 fusion.84
  286.4 1.1 fusion.84
  288.4 1.1 fusion.84
  290.4 1.1 fusion.84
  292.5 1.1 fusion.84
  294.5 1.1 fusion.84
  296.5 1.1 fusion.84
  298.5 1.1 fusion.84
  300.6 1.1 fusion.84
  302.6 1.1 fusion.84
  304.6 1.1 fusion.84
  306.6 1.1 fusion.84
  308.7 1.1 fusion.84
  310.7 1.1 fusion.84
  312.7 1.1 fusion.84
  314.7 1.1 fusion.84
  316.8 1.1 fusion.84
  318.8 32.4 %all-gather.9.cloned.1.call-done = bf16[512,1024]{1,0:T(8,128)(2,1)} async-done(((bf16[32,1024]{1,0:T(8,128)(2,1)}), bf16[512,1024]{1,0:T(8,128)(2,1)}) %all-gather.9.cloned.1.call-update) | async-done | bytes 1048592 | tf_op jit(solution)/shard_map/all_gather | solution.py:123
  351.2 1.7 multiply_reduce_fusion
  353.5 0.5 convolution_convert_fusion
  354.1 1.1 reshape.235
  355.2 4.0 all-to-all-start
  359.1 228.4 %all-gather.11.cloned.1.call-done = bf16[1,1408,2,1024]{3,2,0,1:T(2,128)(2,1)} async-done(((bf16[1,44,2,1024]{3,2,0,1:T(2,128)(2,1)}), bf16[1,1408,2,1024]{3,2,0,1:T(2,128)(2,1)}) %all-gather.11.cloned.1.call-update) | async-done | bytes 5767184 | tf_op jit(solution)/shard_map/all_gather | solution.py:151
  587.5 6.9 copy.188
  594.7 4.7 fusion.14
  599.4 228.0 %all-gather.13.cloned.1.call-done = bf16[1,1408,1024]{2,0,1:T(2,128)(2,1)} async-done(((bf16[1,44,1024]{2,0,1:T(2,128)(2,1)}), bf16[1,1408,1024]{2,0,1:T(2,128)(2,1)}) %all-gather.13.cloned.1.call-update) | async-done | bytes 2883600 | tf_op jit(solution)/shard_map/all_gather | solution.py:152
  827.4 6.6 fusion.16
  834.0 1.1 reshape.237
  835.1 33.9 %all-to-all-start.1 = ((bf16[16,21,1024]{2,1,0:T(8,128)(2,1)}), bf16[16,21,1024]{2,1,0:T(8,128)(2,1)S(1)}, u32[]{:S(2)}, u32[]{:S(2)}) async-start(bf16[16,21,1024]{2,1,0:T(8,128)(2,1)} %reshape.237), calls=%async_computation.1 | async-start | bytes 1572864 | tf_op jit(solution)/shard_map/all_to_all | solution.py:162
  869.7 26.1 %all-to-all-done.1 = bf16[16,21,1024]{2,1,0:T(8,128)(2,1)S(1)} async-done(((bf16[16,21,1024]{2,1,0:T(8,128)(2,1)}), bf16[16,21,1024]{2,1,0:T(8,128)(2,1)S(1)}, u32[]{:S(2)}, u32[]{:S(2)}) %all-to-all-start.1) | async-done | bytes 688160 | tf_op jit(solution)/shard_map/all_to_all | solution.py:162
  896.0 0.5 fusion.19
  896.6 0.7 reshape.240
  897.3 0.7 gather_fusion
  898.0 0.7 bitcast_select_fusion
  (319 shorter events, 35.7 us)
Async XLA Ops:
  7.2 862.3 %copy-start = (bf16[1024,16]{0,1:T(8,128)(2,1)S(1)}, bf16[1024,16]{0,1:T(8,128)(2,1)}, u32[]{:S(2)}) copy-start(bf16[1024,16]{0,1:T(8,128)(2,1)} %param.34) | copy-start | bytes 98308
  7.2 2.6 copy-start.2
  7.2 246.9 %all-gather.7.cloned.1.call-start = ((), (), s32[]{:S(2)}) async-start(), calls=%async_computation.2 | async-start | bytes 8650752 | tf_op jit(solution)/shard_map/all_gather | solution.py:11
  10.4 3.1 copy-start.7
  12.0 226.0 %copy-start.3 = (bf16[2,64,3,512]{3,1,2,0:T(8,128)(2,1)S(1)}, bf16[2,64,3,512]{3,1,2,0:T(8,128)(2,1)}, u32[]{:S(2)}) copy-start(bf16[2,64,3,512]{3,1,2,0:T(8,128)(2,1)} %param.20) | copy-start | bytes 1179652
  12.0 339.2 %all-gather.9.cloned.1.call-start = ((), (), s32[]{:S(2)}) async-start(), calls=%async_computation.3 | async-start | bytes 1114112 | tf_op jit(solution)/shard_map/all_gather | solution.py:123
  12.7 574.8 %all-gather.11.cloned.1.call-start = ((), (), s32[]{:S(2)}) async-start(), calls=%async_computation.4 | async-start | bytes 5947392 | tf_op jit(solution)/shard_map/all_gather | solution.py:151
  13.5 813.9 %all-gather.13.cloned.1.call-start = ((), (), s32[]{:S(2)}) async-start(), calls=%async_computation.5 | async-start | bytes 5947392 | tf_op jit(solution)/shard_map/all_gather | solution.py:152
  14.7 223.7 %copy-start.8 = (s32[2,64,64]{2,1,0:T(8,128)S(1)}, s32[2,64,64]{2,1,0:T(8,128)}, u32[]{:S(2)}) copy-start(s32[2,64,64]{2,1,0:T(8,128)} %param.21) | copy-start | bytes 98308
  14.8 223.8 %copy-start.5 = (bf16[2,128,512]{2,1,0:T(8,128)(2,1)S(1)}, bf16[2,128,512]{2,1,0:T(8,128)(2,1)}, u32[]{:S(2)}) copy-start(bf16[2,128,512]{2,1,0:T(8,128)(2,1)} %param.22) | copy-start | bytes 786436
  133.8 105.0 %copy-start.13 = (s32[2]{0:T(128)S(1)}, s32[2]{0:T(128)}, u32[]{:S(2)}) copy-start(s32[2]{0:T(128)} %param.24) | copy-start | bytes 28
  133.8 105.2 %copy-start.6 = (bf16[2,128,512]{2,1,0:T(8,128)(2,1)S(1)}, bf16[2,128,512]{2,1,0:T(8,128)(2,1)}, u32[]{:S(2)}) copy-start(bf16[2,128,512]{2,1,0:T(8,128)(2,1)} %param.23) | copy-start | bytes 786436
  240.7 0.9 copy-start.10
  240.7 0.9 copy-start.11
  240.7 0.9 copy-start.9
  255.1 96.1 %copy-start.4 = (bf16[128,1024]{1,0:T(8,128)(2,1)S(1)}, bf16[128,1024]{1,0:T(8,128)(2,1)}, u32[]{:S(2)}) copy-start(bf16[128,1024]{1,0:T(8,128)(2,1)} %param.25) | copy-start | bytes 786436
  355.2 239.3 %all-to-all-start = ((bf16[16,21,1024]{2,1,0:T(8,128)(2,1)}), bf16[16,21,1024]{2,1,0:T(8,128)(2,1)S(1)}, u32[]{:S(2)}, u32[]{:S(2)}) async-start(bf16[16,21,1024]{2,1,0:T(8,128)(2,1)} %reshape.235), calls=%async_computation | async-start | bytes 1572864 | tf_op jit(solution)/shard_map/all_to_all | solution.py:149
  834.0 35.3 %copy-start.12 = (s32[2,8]{1,0:T(2,128)S(1)}, s32[2,8]{1,0:T(2,128)}, u32[]{:S(2)}) copy-start(s32[2,8]{1,0:T(2,128)} %param.26) | copy-start | bytes 196
  835.1 60.6 %all-to-all-start.1 = ((bf16[16,21,1024]{2,1,0:T(8,128)(2,1)}), bf16[16,21,1024]{2,1,0:T(8,128)(2,1)S(1)}, u32[]{:S(2)}, u32[]{:S(2)}) async-start(bf16[16,21,1024]{2,1,0:T(8,128)(2,1)} %reshape.237), calls=%async_computation.1 | async-start | bytes 1572864 | tf_op jit(solution)/shard_map/all_to_all | solution.py:162
  896.6 2.1 copy-start.1
Sparse Core Ops, SparseCore 0:
  12.1 241.9 all-gather.6
  257.4 93.7 all-gather.8
  353.3 234.1 all-gather.10
  589.4 237.8 all-gather.12
where the time goes:
time: 907 us; the launch traced here: 905 us
  waiting for transfers between devices  526 us (58%)
  blocking collectives  223 us (25%)
  local copies, waits for them, and re-layouts  46.9 us (5%)
  other arithmetic  38.4 us (4%)
  starting transfers between devices  38 us (4%)
  matrix products  16.9 us (2%)
  between operations  14.3 us (2%)
    all_gather x1, waiting for transfers between devices, on_device(): weight_in = lax.all_gather(expert_in, 'blk', axis=1, tiled=True)[0]  228 us
    all_gather x1, waiting for transfers between devices, on_device(): weight_out = lax.all_gather(expert_out, 'blk', axis=1, tiled=True)[0]  228 us
    all_gather x2, blocking collectives, combined_all(): gathered = jax.tree.map(lambda a: lax.all_gather(a, axis), part)  223 us
    all_to_all x1, starting transfers between devices, on_device(): lax.all_to_all(expert_y, 'expert', split_axis=0, concat_axis=0, tiled=True)  33.9 us
    add x31, other arithmetic, pair_join(): output = expand(former_scale, former[2]) + expand(latter_scale, latter[2])  33.7 us
    all_gather x1, waiting for transfers between devices, on_device(): lax.all_gather(out_weight, 'expert', axis=0, tiled=True)  32.4 us
    all_to_all x1, waiting for transfers between devices, on_device(): lax.all_to_all(expert_y, 'expert', split_axis=0, concat_axis=0, tiled=True)  26.1 us
    mul x127, local copies, waits for them, and re-layouts, expand(): return (shaped * factor[..., None]).reshape(output.shape)  21.2 us
  transfers between devices with their start and end apart: 6, of which 5 were waited for; matrix products, arithmetic and copies ran while one was open for 10% of the time, Pallas kernels for 0%

commit v1 on v0

--- a/solution.py
+++ b/solution.py
@@ -7,14 +7,64 @@
 HD = 64
 
 
-def combined_all(part, axis, combine):
-    gathered = jax.tree.map(lambda a: lax.all_gather(a, axis), part)
-
-    def take(source):
-        return jax.tree.map(lambda a: lax.dynamic_index_in_dim(a, source, 0, False), gathered)
-
-    return lax.fori_loop(
-        1, lax.axis_size(axis), lambda source, state: combine(state, take(source)), take(0)
+def xor_exchange(array, axis, size, bit):
+    return lax.ppermute(array, axis, [(i, i ^ bit) for i in range(size)])
+
+
+def shift_x(array, step):
+    pairs = [(i, ((i // 8 + step) % 4) * 8 + i % 8) for i in range(32)]
+    return lax.ppermute(array, "blk", pairs)
+
+
+def gather_blk(block):
+    for bit in (2, 1):
+        block = jnp.concatenate([block, xor_exchange(block, "blk", 32, bit)], axis=0)
+    half = block.shape[0] // 2
+    before = shift_x(block, 1)
+    after = shift_x(block, -1)
+    far = (shift_x(before[:half], 1), shift_x(after[half:], -1))
+    return (block, before, after) + far
+
+
+def gather_expert(block):
+    rows, columns = block.shape
+    place = lax.axis_index("expert")
+    for axis, bit in enumerate((8, 4, 2, 1)):
+        other = xor_exchange(block, "expert", 16, bit)
+        mine_first = (place // bit) % 2 == 0
+        first = jnp.where(mine_first, block, other)
+        second = jnp.where(mine_first, other, block)
+        block = jnp.stack([first, second], axis=axis)
+    return block.reshape(16 * rows, columns)
+
+
+def scatter_parts(part, share_rows, blocks):
+    peaks, totals, output = part
+    count, tree = peaks.shape[:2]
+    packed = jnp.concatenate([output, peaks, totals], axis=-1)
+    width = packed.shape[-1]
+    packed = packed.reshape(count, tree // share_rows, share_rows, width).transpose(1, 0, 2, 3)
+    arrived = lax.all_to_all(packed, "blk", split_axis=0, concat_axis=0, tiled=True)
+    others = [xor_exchange(block, "blk", 32, 4) for block in blocks]
+    arrived, others = lax.optimization_barrier((arrived, others))
+    pairs = [jnp.concatenate(pair, axis=0) for pair in zip(blocks, others)]
+    wide = output.shape[-1]
+    part = (
+        arrived[..., wide : wide + HEADS],
+        arrived[..., wide + HEADS :],
+        arrived[..., :wide],
+    )
+    return part, pairs
+
+
+def join_many(parts):
+    peaks, totals, output = parts
+    highest = jnp.max(peaks, axis=0)
+    scale = jnp.exp(peaks - highest[None])
+    return (
+        highest,
+        jnp.sum(scale * totals, axis=0),
+        jnp.sum(expand(scale, output), axis=0),
     )
 
 
@@ -102,10 +152,10 @@
     local_part = block_part(long_queries, heads_of(long_keys), heads_of(long_values), everything)
     share_rows = tree_size // lax.axis_size("blk")
     share_start = lax.axis_index("blk") * share_rows
-    merged = combined_all(local_part, "blk", pair_join)
-    cache_part = tuple(
-        (lax.dynamic_slice_in_dim(member, share_start, share_rows, 1) for member in merged)
-    )
+    arrived, weights = scatter_parts(
+        local_part, share_rows, (expert_in[0, :, 0, :], expert_in[0, :, 1, :], expert_out[0])
+    )
+    cache_part = join_many(arrived)
     share_queries = lax.dynamic_slice_in_dim(long_queries, share_start, share_rows, 1)
     share_mask = lax.dynamic_slice_in_dim(long_mask, share_start, share_rows, 1)
     long_tree = block_part(
@@ -120,7 +170,7 @@
     row_count = attn_rows.shape[0]
     projected = jnp.dot(
         attn_rows,
-        lax.all_gather(out_weight, "expert", axis=0, tiled=True),
+        gather_expert(out_weight),
         preferred_element_type=jnp.float32,
     )
     layer_state = (residual.astype(jnp.float32) + projected).astype(jnp.bfloat16)
@@ -148,16 +198,19 @@
     dispatch = dispatch.reshape(expert_count, capacity, model_width)
     received = lax.all_to_all(dispatch, "expert", split_axis=0, concat_axis=0, tiled=True)
     flat_rows = received.reshape(-1, model_width)
-    weight_in = lax.all_gather(expert_in, "blk", axis=1, tiled=True)[0]
-    weight_out = lax.all_gather(expert_out, "blk", axis=1, tiled=True)[0]
-    gate_part = jnp.einsum(
-        "rd,nd->rn", flat_rows, weight_in[:, 0, :], preferred_element_type=jnp.float32
-    )
-    up_part = jnp.einsum(
-        "rd,nd->rn", flat_rows, weight_in[:, 1, :], preferred_element_type=jnp.float32
-    )
-    inner_act = (jax.nn.gelu(gate_part, approximate=True) * up_part).astype(jnp.bfloat16)
-    expert_sum = jnp.dot(inner_act, weight_out, preferred_element_type=jnp.float32)
+    gate_blocks, up_blocks, out_blocks = [gather_blk(block) for block in weights]
+    expert_sum = jnp.zeros((flat_rows.shape[0], model_width), jnp.float32)
+    for gate_block, up_block, out_block in zip(gate_blocks, up_blocks, out_blocks):
+        gate_part = jnp.einsum(
+            "rd,nd->rn", flat_rows, gate_block, preferred_element_type=jnp.float32
+        )
+        up_part = jnp.einsum(
+            "rd,nd->rn", flat_rows, up_block, preferred_element_type=jnp.float32
+        )
+        inner_act = (jax.nn.gelu(gate_part, approximate=True) * up_part).astype(jnp.bfloat16)
+        expert_sum = expert_sum + jnp.dot(
+            inner_act, out_block, preferred_element_type=jnp.float32
+        )
     expert_y = expert_sum.astype(jnp.bfloat16).reshape(expert_count, capacity, model_width)
     returned = lax.all_to_all(expert_y, "expert", split_axis=0, concat_axis=0, tiled=True)
     per_route = jnp.einsum(

time: 907 us -> 304 us (0.34)
  the two profiles are of different devices: /device:TPU:1 before, /device:TPU:32 now
where the time goes in v1:
time: 304 us; the launch traced here: 303 us
  starting transfers between devices  133 us (44%)
  waiting for transfers between devices  116 us (38%)
  matrix products  26.3 us (9%)
  local copies, waits for them, and re-layouts  19.8 us (7%)
  other arithmetic  6.22 us (2%)
    ppermute x13, starting transfers between devices, xor_exchange(): return lax.ppermute(array, axis, [(i, i ^ bit) for i in range(size)])  65.5 us
    ppermute x13, waiting for transfers between devices, xor_exchange(): return lax.ppermute(array, axis, [(i, i ^ bit) for i in range(size)])  52.1 us
    all_to_all x1, waiting for transfers between devices, on_device(): lax.all_to_all(expert_y, 'expert', split_axis=0, concat_axis=0, tiled=True)  46.5 us
    ppermute x12, starting transfers between devices, shift_x(): return lax.ppermute(array, 'blk', pairs)  38.3 us
    ppermute x12, waiting for transfers between devices, shift_x(): return lax.ppermute(array, 'blk', pairs)  17.3 us
    dot_general x5, matrix products, on_device(): jnp.dot(inner_act, out_block, preferred_element_type=jnp.float32)  15.1 us
    all_to_all x1, starting transfers between devices, on_device(): lax.all_to_all(expert_y, 'expert', split_axis=0, concat_axis=0, tiled=True)  13.5 us
    all_to_all x1, starting transfers between devices, scatter_parts(): lax.all_to_all(packed, 'blk', split_axis=0, concat_axis=0, tiled=True)  9.94 us
  transfers between devices with their start and end apart: 28, of which 12 were waited for; matrix products, arithmetic and copies ran while one was open for 12% of the time, Pallas kernels for 0%

profile of v1, /device:TPU:32, one launch (start us, length us, event | category | flops | bytes accessed | tf_op | source)
XLA Modules:
  0.0 302.8 jit_solution(15170996784969313290)
XLA Ops:
  0.7 15.0 %collective-permute-start.3 = (bf16[32,1024]{1,0:T(8,128)(2,1)}, bf16[32,1024]{1,0:T(8,128)(2,1)}, u32[]{:S(2)}, u32[]{:S(2)}) collective-permute-start(bf16[32,1024]{1,0:T(8,128)(2,1)} %param.30), channel_id=1, source_target_pairs={{0,8},{1,9},{2,10},{3,11},{4,12},{5,13},{6,14},{7,15},{8,0},{9,1},... | collective-permute-start | bytes 196616 | tf_op jit(solution)/shard_map/ppermute | solution.py:11
  15.6 4.3 %collective-permute-start.2 = (bf16[44,1024]{1,0:T(8,128)(2,1)}, bf16[44,1024]{1,0:T(8,128)(2,1)S(1)}, u32[]{:S(2)}, u32[]{:S(2)}) collective-permute-start(bf16[44,1024]{1,0:T(8,128)(2,1)} %bitcast.171), channel_id=1, source_target_pairs={{0,64},{16,80},{32,96},{48,112},{64,0},{80,16},{96,32},{112,48},{1... | collective-permute-start | bytes 270344 | tf_op jit(solution)/shard_map/ppermute | solution.py:11
  19.9 1.3 fusion.147
  21.3 5.5 %collective-permute-start = (bf16[44,1024]{1,0:T(8,128)(2,1)S(1)}, bf16[44,1024]{1,0:T(8,128)(2,1)S(1)}, u32[]{:S(2)}, u32[]{:S(2)}) collective-permute-start(bf16[44,1024]{1,0:T(8,128)(2,1)S(1)} %bitcast.165), channel_id=1, source_target_pairs={{0,64},{16,80},{32,96},{48,112},{64,0},{80,16},{96,32},{112,48},{1... | collective-permute-start | bytes 270344 | tf_op jit(solution)/shard_map/ppermute | solution.py:11
  26.8 4.3 %collective-permute-start.1 = (bf16[44,1024]{1,0:T(8,128)(2,1)S(1)}, bf16[44,1024]{1,0:T(8,128)(2,1)S(1)}, u32[]{:S(2)}, u32[]{:S(2)}) collective-permute-start(bf16[44,1024]{1,0:T(8,128)(2,1)S(1)} %bitcast.161), channel_id=1, source_target_pairs={{0,64},{16,80},{32,96},{48,112},{64,0},{80,16},{96,32},{112,48},{1... | collective-permute-start | bytes 270344 | tf_op jit(solution)/shard_map/ppermute | solution.py:11
  31.1 0.7 fusion.146
  34.7 0.8 copy.231
  35.4 9.9 %all-to-all-start = ((f32[32,2,2,528]{3,2,1,0:T(2,128)}), f32[32,2,2,528]{3,2,1,0:T(2,128)S(1)}, u32[]{:S(2)}, u32[]{:S(2)}) async-start(f32[32,2,2,528]{3,2,1,0:T(2,128)} %copy.231), calls=%async_computation | async-start | bytes 655360 | tf_op jit(solution)/shard_map/all_to_all | solution.py:47
  47.2 0.7 dynamic-slice_compare_fusion
  50.6 0.9 select_bitcast_fusion.7
  51.5 5.1 %collective-permute-start.4 = (bf16[2,32,1024]{2,1,0:T(8,128)(2,1)S(1)}, bf16[2,32,1024]{2,1,0:T(8,128)(2,1)S(1)}, u32[]{:S(2)}, u32[]{:S(2)}) collective-permute-start(bf16[2,32,1024]{2,1,0:T(8,128)(2,1)S(1)} %pad_maximum_fusion.12), channel_id=1, source_target_pairs={{0,4},{1,5},{2,6},{3,7},{4,0},{5,1},{6,2},{7,3},{8,12},{9,13},{10,... | collective-permute-start | bytes 393224 | tf_op jit(solution)/shard_map/ppermute | solution.py:11
  56.6 0.9 reduce-window.6
  57.7 2.2 collective-permute-done.4
  59.9 3.5 %collective-permute-start.5 = (bf16[2,2,32,1024]{3,2,1,0:T(8,128)(2,1)S(1)}, bf16[2,2,32,1024]{3,2,1,0:T(8,128)(2,1)S(1)}, u32[]{:S(2)}, u32[]{:S(2)}) collective-permute-start(bf16[2,2,32,1024]{3,2,1,0:T(8,128)(2,1)S(1)} %pad_maximum_fusion.8), channel_id=1, source_target_pairs={{0,2},{1,3},{2,0},{3,1},{4,6},{5,7},{6,4},{7,5},{8,10},{9,11},{10,... | collective-permute-start | bytes 786440 | tf_op jit(solution)/shard_map/ppermute | solution.py:11
  64.5 3.6 %collective-permute-done.5 = bf16[2,2,32,1024]{3,2,1,0:T(8,128)(2,1)S(1)} collective-permute-done((bf16[2,2,32,1024]{3,2,1,0:T(8,128)(2,1)S(1)}, bf16[2,2,32,1024]{3,2,1,0:T(8,128)(2,1)S(1)}, u32[]{:S(2)}, u32[]{:S(2)}) %collective-permute-start.5) | collective-permute-done | bytes 262176 | tf_op jit(solution)/shard_map/ppermute | solution.py:11
  68.3 1.9 collective-permute-start.6
  70.5 1.6 collective-permute-done.6
  73.8 0.8 copy-done.1
  76.5 1.2 reshape.232
  77.7 5.6 %all-to-all-start.1 = ((bf16[16,21,1024]{2,1,0:T(8,128)(2,1)}), bf16[16,21,1024]{2,1,0:T(8,128)(2,1)S(1)}, u32[]{:S(2)}, u32[]{:S(2)}) async-start(bf16[16,21,1024]{2,1,0:T(8,128)(2,1)} %reshape.232), calls=%async_computation.1 | async-start | bytes 1572864 | tf_op jit(solution)/shard_map/all_to_all | solution.py:199
  83.3 4.3 %collective-permute-start.7 = (bf16[88,1024]{1,0:T(8,128)(2,1)S(1)}, bf16[88,1024]{1,0:T(8,128)(2,1)S(1)}, u32[]{:S(2)}, u32[]{:S(2)}) collective-permute-start(bf16[88,1024]{1,0:T(8,128)(2,1)S(1)} %pad_maximum_fusion.9), channel_id=1, source_target_pairs={{0,32},{16,48},{32,0},{48,16},{64,96},{80,112},{96,64},{112,80},{1... | collective-permute-start | bytes 540680 | tf_op jit(solution)/shard_map/ppermute | solution.py:11
  87.6 35.9 %collective-permute-done.7 = bf16[88,1024]{1,0:T(8,128)(2,1)S(1)} collective-permute-done((bf16[88,1024]{1,0:T(8,128)(2,1)S(1)}, bf16[88,1024]{1,0:T(8,128)(2,1)S(1)}, u32[]{:S(2)}, u32[]{:S(2)}) %collective-permute-start.7) | collective-permute-done | bytes 180256 | tf_op jit(solution)/shard_map/ppermute | solution.py:11
  123.5 8.5 %collective-permute-start.8 = (bf16[176,1024]{1,0:T(8,128)(2,1)S(1)}, bf16[176,1024]{1,0:T(8,128)(2,1)S(1)}, u32[]{:S(2)}, u32[]{:S(2)}) collective-permute-start(bf16[176,1024]{1,0:T(8,128)(2,1)S(1)} %pad_maximum_fusion.5), channel_id=1, source_target_pairs={{0,16},{16,0},{32,48},{48,32},{64,80},{80,64},{96,112},{112,96},{1... | collective-permute-start | bytes 1081352 | tf_op jit(solution)/shard_map/ppermute | solution.py:11
  132.1 1.9 collective-permute-start.9
  134.1 4.8 %collective-permute-start.11 = (bf16[88,1024]{1,0:T(8,128)(2,1)S(1)}, bf16[88,1024]{1,0:T(8,128)(2,1)S(1)}, u32[]{:S(2)}, u32[]{:S(2)}) collective-permute-start(bf16[88,1024]{1,0:T(8,128)(2,1)S(1)} %pad_maximum_fusion.11), channel_id=1, source_target_pairs={{0,32},{16,48},{32,0},{48,16},{64,96},{80,112},{96,64},{112,80},{1... | collective-permute-start | bytes 540680 | tf_op jit(solution)/shard_map/ppermute | solution.py:11
  138.9 4.9 %collective-permute-done.8 = bf16[176,1024]{1,0:T(8,128)(2,1)S(1)} collective-permute-done((bf16[176,1024]{1,0:T(8,128)(2,1)S(1)}, bf16[176,1024]{1,0:T(8,128)(2,1)S(1)}, u32[]{:S(2)}, u32[]{:S(2)}) %collective-permute-start.8) | collective-permute-done | bytes 360480 | tf_op jit(solution)/shard_map/ppermute | solution.py:11
  143.9 4.6 %collective-permute-start.16 = (bf16[352,1024]{1,0:T(8,128)(2,1)S(1)}, bf16[352,1024]{1,0:T(8,128)(2,1)S(1)}, u32[]{:S(2)}, u32[]{:S(2)}) collective-permute-start(bf16[352,1024]{1,0:T(8,128)(2,1)S(1)} %pad_maximum_fusion.1), channel_id=1, source_target_pairs={{0,384},{16,400},{32,416},{48,432},{64,448},{80,464},{96,480},{112... | collective-permute-start | bytes 2162696 | tf_op jit(solution)/shard_map/ppermute | solution.py:16
  148.6 4.6 %collective-permute-start.10 = (bf16[176,1024]{1,0:T(8,128)(2,1)S(1)}, bf16[176,1024]{1,0:T(8,128)(2,1)S(1)}, u32[]{:S(2)}, u32[]{:S(2)}) collective-permute-start(bf16[176,1024]{1,0:T(8,128)(2,1)S(1)} %pad_maximum_fusion.6), channel_id=1, source_target_pairs={{0,16},{16,0},{32,48},{48,32},{64,80},{80,64},{96,112},{112,96},{1... | collective-permute-start | bytes 1081352 | tf_op jit(solution)/shard_map/ppermute | solution.py:11
  153.3 1.9 collective-permute-start.12
  155.2 3.3 %collective-permute-start.13 = (bf16[352,1024]{1,0:T(8,128)(2,1)S(1)}, bf16[352,1024]{1,0:T(8,128)(2,1)S(1)}, u32[]{:S(2)}, u32[]{:S(2)}) collective-permute-start(bf16[352,1024]{1,0:T(8,128)(2,1)S(1)} %pad_maximum_fusion.1), channel_id=1, source_target_pairs={{0,128},{16,144},{32,160},{48,176},{64,192},{80,208},{96,224},{112... | collective-permute-start | bytes 2162696 | tf_op jit(solution)/shard_map/ppermute | solution.py:16
  158.5 3.8 %collective-permute-done.10 = bf16[176,1024]{1,0:T(8,128)(2,1)S(1)} collective-permute-done((bf16[176,1024]{1,0:T(8,128)(2,1)S(1)}, bf16[176,1024]{1,0:T(8,128)(2,1)S(1)}, u32[]{:S(2)}, u32[]{:S(2)}) %collective-permute-start.10) | collective-permute-done | bytes 360480 | tf_op jit(solution)/shard_map/ppermute | solution.py:11
  162.4 3.7 %collective-permute-start.17 = (bf16[352,1024]{1,0:T(8,128)(2,1)S(1)}, bf16[352,1024]{1,0:T(8,128)(2,1)S(1)}, u32[]{:S(2)}, u32[]{:S(2)}) collective-permute-start(bf16[352,1024]{1,0:T(8,128)(2,1)S(1)} %pad_maximum_fusion.2), channel_id=1, source_target_pairs={{0,384},{16,400},{32,416},{48,432},{64,448},{80,464},{96,480},{112... | collective-permute-start | bytes 2162696 | tf_op jit(solution)/shard_map/ppermute | solution.py:16
  166.1 2.2 collective-permute-start.14
  168.3 4.9 %collective-permute-start.18 = (bf16[352,1024]{1,0:T(8,128)(2,1)S(1)}, bf16[352,1024]{1,0:T(8,128)(2,1)S(1)}, u32[]{:S(2)}, u32[]{:S(2)}) collective-permute-start(bf16[352,1024]{1,0:T(8,128)(2,1)S(1)} %pad_maximum_fusion.3), channel_id=1, source_target_pairs={{0,384},{16,400},{32,416},{48,432},{64,448},{80,464},{96,480},{112... | collective-permute-start | bytes 2162696 | tf_op jit(solution)/shard_map/ppermute | solution.py:16
  173.2 1.9 collective-permute-start.15
  175.2 0.8 slice.95
  175.9 1.4 collective-permute-done.13
  177.3 3.8 %collective-permute-start.22 = (bf16[176,1024]{1,0:T(8,128)(2,1)}, bf16[176,1024]{1,0:T(8,128)(2,1)S(1)}, u32[]{:S(2)}, u32[]{:S(2)}) collective-permute-start(bf16[176,1024]{1,0:T(8,128)(2,1)} %slice.95), channel_id=1, source_target_pairs={{0,384},{16,400},{32,416},{48,432},{64,448},{80,464},{96,480},{112... | collective-permute-start | bytes 1081352 | tf_op jit(solution)/shard_map/ppermute | solution.py:16
  181.1 0.8 slice.92
  181.8 1.4 collective-permute-done.17
  183.3 2.4 collective-permute-start.19
  185.7 0.8 slice.96
  186.5 6.3 %collective-permute-done.14 = bf16[352,1024]{1,0:T(8,128)(2,1)S(1)} collective-permute-done((bf16[352,1024]{1,0:T(8,128)(2,1)S(1)}, bf16[352,1024]{1,0:T(8,128)(2,1)S(1)}, u32[]{:S(2)}, u32[]{:S(2)}) %collective-permute-start.14) | collective-permute-done | bytes 720928 | tf_op jit(solution)/shard_map/ppermute | solution.py:16
  192.8 3.3 %collective-permute-start.23 = (bf16[176,1024]{1,0:T(8,128)(2,1)}, bf16[176,1024]{1,0:T(8,128)(2,1)}, u32[]{:S(2)}, u32[]{:S(2)}) collective-permute-start(bf16[176,1024]{1,0:T(8,128)(2,1)} %slice.96), channel_id=1, source_target_pairs={{0,384},{16,400},{32,416},{48,432},{64,448},{80,464},{96,480},{112... | collective-permute-start | bytes 1081352 | tf_op jit(solution)/shard_map/ppermute | solution.py:16
  196.1 0.8 slice.93
  196.8 1.9 collective-permute-done.18
  198.7 2.4 collective-permute-start.20
  201.1 0.8 slice.97
  201.9 6.3 %collective-permute-done.15 = bf16[352,1024]{1,0:T(8,128)(2,1)S(1)} collective-permute-done((bf16[352,1024]{1,0:T(8,128)(2,1)S(1)}, bf16[352,1024]{1,0:T(8,128)(2,1)S(1)}, u32[]{:S(2)}, u32[]{:S(2)}) %collective-permute-start.15) | collective-permute-done | bytes 720928 | tf_op jit(solution)/shard_map/ppermute | solution.py:16
  208.2 3.3 %collective-permute-start.24 = (bf16[176,1024]{1,0:T(8,128)(2,1)}, bf16[176,1024]{1,0:T(8,128)(2,1)}, u32[]{:S(2)}, u32[]{:S(2)}) collective-permute-start(bf16[176,1024]{1,0:T(8,128)(2,1)} %slice.97), channel_id=1, source_target_pairs={{0,384},{16,400},{32,416},{48,432},{64,448},{80,464},{96,480},{112... | collective-permute-start | bytes 1081352 | tf_op jit(solution)/shard_map/ppermute | solution.py:16
  211.6 0.8 slice.94
  212.6 1.4 fusion.162
  213.9 2.5 collective-permute-start.21
  216.5 1.1 fusion.166
  218.2 2.0 fusion.96
  220.2 1.6 fusion.163
  221.8 3.4 %fusion.73 = f32[336,1024]{1,0:T(8,128)} fusion(bf16[352,1024]{1,0:T(8,128)(2,1)} %copy-done.11, f32[336,352]{1,0:T(8,128)S(1)} %fusion.164, bf16[336,1024]{1,0:T(8,128)(2,1)S(1)} %reshape.233, bf16[352,1024]{1,0:T(8,128)(2,1)} %copy-done.9), kind=kOutput, calls=%fused_computation.117 | convolution fusion | flops 485624832 | bytes 3979264 | tf_op jit(solution)/shard_map/dot_general | solution.py:211
  225.3 2.1 fusion.165
  227.4 3.5 %fusion.75 = f32[336,1024]{1,0:T(8,128)} fusion(bf16[352,1024]{1,0:T(8,128)(2,1)} %copy-done.10, f32[336,352]{1,0:T(8,128)S(1)} %fusion.163, bf16[336,1024]{1,0:T(8,128)(2,1)S(1)} %reshape.233, bf16[352,1024]{1,0:T(8,128)(2,1)} %copy-done.8), kind=kOutput, calls=%fused_computation.118 | convolution fusion | flops 485624832 | bytes 3979264 | tf_op jit(solution)/shard_map/dot_general | solution.py:211
  230.9 2.0 fusion.98
  232.9 4.2 %fusion.4 = bf16[336,1024]{1,0:T(8,128)(2,1)} fusion(f32[336,1024]{1,0:T(8,128)S(1)} %fusion.96, f32[336,1024]{1,0:T(8,128)S(1)} %fusion.98, f32[336,1024]{1,0:T(8,128)} %fusion.73, f32[336,1024]{1,0:T(8,128)} %fusion.75, bf16[352,1024]{1,0:T(8,128)(2,1)} %copy-done.4, f32[336,352]{1,0:T(8,128)} %fusion.162, bf16[336,1024]{1,0:T(8,128)(2,1)S(1)} %reshape.233, ...), kind=kOutput, calls=%fused_computation.8 | convolution fusion | flops 487345152 | bytes 8796160 | tf_op jit(solution)/shard_map/dot_general | solution.py:211
  237.1 2.3 reshape.234
  239.4 13.5 %all-to-all-start.2 = ((bf16[16,21,1024]{2,1,0:T(8,128)(2,1)}), bf16[16,21,1024]{2,1,0:T(8,128)(2,1)S(1)}, u32[]{:S(2)}, u32[]{:S(2)}) async-start(bf16[16,21,1024]{2,1,0:T(8,128)(2,1)} %reshape.234), calls=%async_computation.2 | async-start | bytes 1572864 | tf_op jit(solution)/shard_map/all_to_all | solution.py:215
  253.5 46.5 %all-to-all-done.2 = bf16[16,21,1024]{2,1,0:T(8,128)(2,1)S(1)} async-done(((bf16[16,21,1024]{2,1,0:T(8,128)(2,1)}), bf16[16,21,1024]{2,1,0:T(8,128)(2,1)S(1)}, u32[]{:S(2)}, u32[]{:S(2)}) %all-to-all-start.2) | async-done | bytes 688160 | tf_op jit(solution)/shard_map/all_to_all | solution.py:215
  (173 shorter events, 16.8 us)
Async XLA Ops:
  0.6 252.7 %copy-start = (bf16[1024,16]{0,1:T(8,128)(2,1)S(1)}, bf16[1024,16]{0,1:T(8,128)(2,1)}, u32[]{:S(2)}) copy-start(bf16[1024,16]{0,1:T(8,128)(2,1)} %param.32) | copy-start | bytes 98308
  0.6 30.5 %copy-start.18 = (bf16[2,64,3,512]{3,1,2,0:T(8,128)(2,1)S(1)}, bf16[2,64,3,512]{3,1,2,0:T(8,128)(2,1)}, u32[]{:S(2)}) copy-start(bf16[2,64,3,512]{3,1,2,0:T(8,128)(2,1)} %param.25) | copy-start | bytes 1179652
  0.7 31.4 %copy-start.14 = (bf16[2,256,512]{2,1,0:T(8,128)(2,1)S(1)}, bf16[2,256,512]{2,1,0:T(8,128)(2,1)}, u32[]{:S(2)}) copy-start(bf16[2,256,512]{2,1,0:T(8,128)(2,1)} %param.27) | copy-start | bytes 1572868
  0.7 49.7 %collective-permute-start.3 = (bf16[32,1024]{1,0:T(8,128)(2,1)}, bf16[32,1024]{1,0:T(8,128)(2,1)}, u32[]{:S(2)}, u32[]{:S(2)}) collective-permute-start(bf16[32,1024]{1,0:T(8,128)(2,1)} %param.30), channel_id=1, source_target_pairs={{0,8},{1,9},{2,10},{3,11},{4,12},{5,13},{6,14},{7,15},{8,0},{9,1},... | collective-permute-start | bytes 196616 | tf_op jit(solution)/shard_map/ppermute | solution.py:11
  15.6 56.7 %collective-permute-start.2 = (bf16[44,1024]{1,0:T(8,128)(2,1)}, bf16[44,1024]{1,0:T(8,128)(2,1)S(1)}, u32[]{:S(2)}, u32[]{:S(2)}) collective-permute-start(bf16[44,1024]{1,0:T(8,128)(2,1)} %bitcast.171), channel_id=1, source_target_pairs={{0,64},{16,80},{32,96},{48,112},{64,0},{80,16},{96,32},{112,48},{1... | collective-permute-start | bytes 270344 | tf_op jit(solution)/shard_map/ppermute | solution.py:11
  21.3 51.0 %collective-permute-start = (bf16[44,1024]{1,0:T(8,128)(2,1)S(1)}, bf16[44,1024]{1,0:T(8,128)(2,1)S(1)}, u32[]{:S(2)}, u32[]{:S(2)}) collective-permute-start(bf16[44,1024]{1,0:T(8,128)(2,1)S(1)} %bitcast.165), channel_id=1, source_target_pairs={{0,64},{16,80},{32,96},{48,112},{64,0},{80,16},{96,32},{112,48},{1... | collective-permute-start | bytes 270344 | tf_op jit(solution)/shard_map/ppermute | solution.py:11
  26.8 45.5 %collective-permute-start.1 = (bf16[44,1024]{1,0:T(8,128)(2,1)S(1)}, bf16[44,1024]{1,0:T(8,128)(2,1)S(1)}, u32[]{:S(2)}, u32[]{:S(2)}) collective-permute-start(bf16[44,1024]{1,0:T(8,128)(2,1)S(1)} %bitcast.161), channel_id=1, source_target_pairs={{0,64},{16,80},{32,96},{48,112},{64,0},{80,16},{96,32},{112,48},{1... | collective-permute-start | bytes 270344 | tf_op jit(solution)/shard_map/ppermute | solution.py:11
  32.2 1.0 copy-start.15
  34.4 11.1 %copy-start.29 = (s32[2]{0:T(128)S(1)}, s32[2]{0:T(128)}, u32[]{:S(2)}) copy-start(s32[2]{0:T(128)} %param.22) | copy-start | bytes 28
  34.4 11.1 %copy-start.23 = (s32[2,64,64]{2,1,0:T(8,128)S(1)}, s32[2,64,64]{2,1,0:T(8,128)}, u32[]{:S(2)}) copy-start(s32[2,64,64]{2,1,0:T(8,128)} %param.19) | copy-start | bytes 98308
  34.4 11.2 %copy-start.25 = (s32[132,2]{0,1:T(2,128)S(1)}, s32[132,2]{0,1:T(2,128)}, u32[]{:S(2)}) copy-start(s32[132,2]{0,1:T(2,128)} %param.33) | copy-start | bytes 3172
  34.4 11.5 %copy-start.21 = (bf16[2,128,512]{2,1,0:T(8,128)(2,1)S(1)}, bf16[2,128,512]{2,1,0:T(8,128)(2,1)}, u32[]{:S(2)}) copy-start(bf16[2,128,512]{2,1,0:T(8,128)(2,1)} %param.20) | copy-start | bytes 786436
  34.6 11.5 %copy-start.22 = (bf16[2,128,512]{2,1,0:T(8,128)(2,1)S(1)}, bf16[2,128,512]{2,1,0:T(8,128)(2,1)}, u32[]{:S(2)}) copy-start(bf16[2,128,512]{2,1,0:T(8,128)(2,1)} %param.21) | copy-start | bytes 786436
  35.4 10.9 %copy-start.19 = (bf16[2,64,3,512]{3,1,2,0:T(8,128)(2,1)S(1)}, bf16[2,64,3,512]{3,1,2,0:T(8,128)(2,1)}, u32[]{:S(2)}) copy-start(bf16[2,64,3,512]{3,1,2,0:T(8,128)(2,1)} %param.18) | copy-start | bytes 1179652
  35.4 36.9 %all-to-all-start = ((f32[32,2,2,528]{3,2,1,0:T(2,128)}), f32[32,2,2,528]{3,2,1,0:T(2,128)S(1)}, u32[]{:S(2)}, u32[]{:S(2)}) async-start(f32[32,2,2,528]{3,2,1,0:T(2,128)} %copy.231), calls=%async_computation | async-start | bytes 655360 | tf_op jit(solution)/shard_map/all_to_all | solution.py:47
  46.1 0.9 copy-start.17
  49.8 0.9 copy-start.24
  50.3 13.5 %copy-start.27 = (bf16[1024]{0:T(1024)(128)(2,1)S(1)}, bf16[1024]{0:T(1024)(128)(2,1)}, u32[]{:S(2)}) copy-start(bf16[1024]{0:T(1024)(128)(2,1)} %param.31) | copy-start | bytes 6148
  50.3 13.5 %copy-start.26 = (bf16[2,2,1024]{2,1,0:T(2,128)(2,1)S(1)}, bf16[2,2,1024]{2,1,0:T(2,128)(2,1)}, u32[]{:S(2)}) copy-start(bf16[2,2,1024]{2,1,0:T(2,128)(2,1)} %param.29) | copy-start | bytes 24580
  50.3 13.8 %copy-start.16 = (bf16[2,64,1,512]{3,1,2,0:T(8,128)(2,1)S(1)}, bf16[2,64,1,512]{3,1,2,0:T(8,128)(2,1)}, u32[]{:S(2)}) copy-start(bf16[2,64,1,512]{3,1,2,0:T(8,128)(2,1)} %get-tuple-element.27) | copy-start | bytes 393220
  51.5 8.4 %collective-permute-start.4 = (bf16[2,32,1024]{2,1,0:T(8,128)(2,1)S(1)}, bf16[2,32,1024]{2,1,0:T(8,128)(2,1)S(1)}, u32[]{:S(2)}, u32[]{:S(2)}) collective-permute-start(bf16[2,32,1024]{2,1,0:T(8,128)(2,1)S(1)} %pad_maximum_fusion.12), channel_id=1, source_target_pairs={{0,4},{1,5},{2,6},{3,7},{4,0},{5,1},{6,2},{7,3},{8,12},{9,13},{10,... | collective-permute-start | bytes 393224 | tf_op jit(solution)/shard_map/ppermute | solution.py:11
  59.9 8.3 %collective-permute-start.5 = (bf16[2,2,32,1024]{3,2,1,0:T(8,128)(2,1)S(1)}, bf16[2,2,32,1024]{3,2,1,0:T(8,128)(2,1)S(1)}, u32[]{:S(2)}, u32[]{:S(2)}) collective-permute-start(bf16[2,2,32,1024]{3,2,1,0:T(8,128)(2,1)S(1)} %pad_maximum_fusion.8), channel_id=1, source_target_pairs={{0,2},{1,3},{2,0},{3,1},{4,6},{5,7},{6,4},{7,5},{8,10},{9,11},{10,... | collective-permute-start | bytes 786440 | tf_op jit(solution)/shard_map/ppermute | solution.py:11
  68.3 3.8 %collective-permute-start.6 = (bf16[2,2,2,32,1024]{4,3,2,1,0:T(8,128)(2,1)S(1)}, bf16[2,2,2,32,1024]{4,3,2,1,0:T(8,128)(2,1)S(1)}, u32[]{:S(2)}, u32[]{:S(2)}) collective-permute-start(bf16[2,2,2,32,1024]{4,3,2,1,0:T(8,128)(2,1)S(1)} %pad_maximum_fusion.4), channel_id=1, source_target_pairs={{0,1},{1,0},{2,3},{3,2},{4,5},{5,4},{6,7},{7,6},{8,9},{9,8},{10,11... | collective-permute-start | bytes 1572872 | tf_op jit(solution)/shard_map/ppermute | solution.py:11
  72.3 1.1 copy-start.20
  73.8 0.8 copy-start.1
  74.8 0.7 copy-start.5
  77.7 56.4 %copy-start.13 = (bf16[1,44,1024]{2,1,0:T(8,128)(2,1)S(1)}, bf16[1,44,1024]{2,1,0:T(8,128)(2,1)}, u32[]{:S(2)}) copy-start(bf16[1,44,1024]{2,1,0:T(8,128)(2,1)} %param.35) | copy-start | bytes 270340
  77.7 134.7 %all-to-all-start.1 = ((bf16[16,21,1024]{2,1,0:T(8,128)(2,1)}), bf16[16,21,1024]{2,1,0:T(8,128)(2,1)S(1)}, u32[]{:S(2)}, u32[]{:S(2)}) async-start(bf16[16,21,1024]{2,1,0:T(8,128)(2,1)} %reshape.232), calls=%async_computation.1 | async-start | bytes 1572864 | tf_op jit(solution)/shard_map/all_to_all | solution.py:199
  83.3 40.2 %collective-permute-start.7 = (bf16[88,1024]{1,0:T(8,128)(2,1)S(1)}, bf16[88,1024]{1,0:T(8,128)(2,1)S(1)}, u32[]{:S(2)}, u32[]{:S(2)}) collective-permute-start(bf16[88,1024]{1,0:T(8,128)(2,1)S(1)} %pad_maximum_fusion.9), channel_id=1, source_target_pairs={{0,32},{16,48},{32,0},{48,16},{64,96},{80,112},{96,64},{112,80},{1... | collective-permute-start | bytes 540680 | tf_op jit(solution)/shard_map/ppermute | solution.py:11
  123.5 20.3 %collective-permute-start.8 = (bf16[176,1024]{1,0:T(8,128)(2,1)S(1)}, bf16[176,1024]{1,0:T(8,128)(2,1)S(1)}, u32[]{:S(2)}, u32[]{:S(2)}) collective-permute-start(bf16[176,1024]{1,0:T(8,128)(2,1)S(1)} %pad_maximum_fusion.5), channel_id=1, source_target_pairs={{0,16},{16,0},{32,48},{48,32},{64,80},{80,64},{96,112},{112,96},{1... | collective-permute-start | bytes 1081352 | tf_op jit(solution)/shard_map/ppermute | solution.py:11
  132.1 16.5 %collective-permute-start.9 = (bf16[88,1024]{1,0:T(8,128)(2,1)S(1)}, bf16[88,1024]{1,0:T(8,128)(2,1)S(1)}, u32[]{:S(2)}, u32[]{:S(2)}) collective-permute-start(bf16[88,1024]{1,0:T(8,128)(2,1)S(1)} %pad_maximum_fusion.10), channel_id=1, source_target_pairs={{0,32},{16,48},{32,0},{48,16},{64,96},{80,112},{96,64},{112,80},{1... | collective-permute-start | bytes 540680 | tf_op jit(solution)/shard_map/ppermute | solution.py:11
  134.1 19.1 %collective-permute-start.11 = (bf16[88,1024]{1,0:T(8,128)(2,1)S(1)}, bf16[88,1024]{1,0:T(8,128)(2,1)S(1)}, u32[]{:S(2)}, u32[]{:S(2)}) collective-permute-start(bf16[88,1024]{1,0:T(8,128)(2,1)S(1)} %pad_maximum_fusion.11), channel_id=1, source_target_pairs={{0,32},{16,48},{32,0},{48,16},{64,96},{80,112},{96,64},{112,80},{1... | collective-permute-start | bytes 540680 | tf_op jit(solution)/shard_map/ppermute | solution.py:11
  143.9 29.3 %collective-permute-start.16 = (bf16[352,1024]{1,0:T(8,128)(2,1)S(1)}, bf16[352,1024]{1,0:T(8,128)(2,1)S(1)}, u32[]{:S(2)}, u32[]{:S(2)}) collective-permute-start(bf16[352,1024]{1,0:T(8,128)(2,1)S(1)} %pad_maximum_fusion.1), channel_id=1, source_target_pairs={{0,384},{16,400},{32,416},{48,432},{64,448},{80,464},{96,480},{112... | collective-permute-start | bytes 2162696 | tf_op jit(solution)/shard_map/ppermute | solution.py:16
  148.6 13.6 %collective-permute-start.10 = (bf16[176,1024]{1,0:T(8,128)(2,1)S(1)}, bf16[176,1024]{1,0:T(8,128)(2,1)S(1)}, u32[]{:S(2)}, u32[]{:S(2)}) collective-permute-start(bf16[176,1024]{1,0:T(8,128)(2,1)S(1)} %pad_maximum_fusion.6), channel_id=1, source_target_pairs={{0,16},{16,0},{32,48},{48,32},{64,80},{80,64},{96,112},{112,96},{1... | collective-permute-start | bytes 1081352 | tf_op jit(solution)/shard_map/ppermute | solution.py:11
  153.3 15.0 %collective-permute-start.12 = (bf16[176,1024]{1,0:T(8,128)(2,1)S(1)}, bf16[176,1024]{1,0:T(8,128)(2,1)S(1)}, u32[]{:S(2)}, u32[]{:S(2)}) collective-permute-start(bf16[176,1024]{1,0:T(8,128)(2,1)S(1)} %pad_maximum_fusion.7), channel_id=1, source_target_pairs={{0,16},{16,0},{32,48},{48,32},{64,80},{80,64},{96,112},{112,96},{1... | collective-permute-start | bytes 1081352 | tf_op jit(solution)/shard_map/ppermute | solution.py:11
  155.2 22.1 %collective-permute-start.13 = (bf16[352,1024]{1,0:T(8,128)(2,1)S(1)}, bf16[352,1024]{1,0:T(8,128)(2,1)S(1)}, u32[]{:S(2)}, u32[]{:S(2)}) collective-permute-start(bf16[352,1024]{1,0:T(8,128)(2,1)S(1)} %pad_maximum_fusion.1), channel_id=1, source_target_pairs={{0,128},{16,144},{32,160},{48,176},{64,192},{80,208},{96,224},{112... | collective-permute-start | bytes 2162696 | tf_op jit(solution)/shard_map/ppermute | solution.py:16
  162.4 49.2 %copy-start.3 = (bf16[352,1024]{1,0:T(8,128)(2,1)}, bf16[352,1024]{1,0:T(8,128)(2,1)S(1)}, u32[]{:S(2)}) copy-start(bf16[352,1024]{1,0:T(8,128)(2,1)S(1)} %pad_maximum_fusion.2) | copy-start | bytes 2162692
  162.4 20.9 %collective-permute-start.17 = (bf16[352,1024]{1,0:T(8,128)(2,1)S(1)}, bf16[352,1024]{1,0:T(8,128)(2,1)S(1)}, u32[]{:S(2)}, u32[]{:S(2)}) collective-permute-start(bf16[352,1024]{1,0:T(8,128)(2,1)S(1)} %pad_maximum_fusion.2), channel_id=1, source_target_pairs={{0,384},{16,400},{32,416},{48,432},{64,448},{80,464},{96,480},{112... | collective-permute-start | bytes 2162696 | tf_op jit(solution)/shard_map/ppermute | solution.py:16
  166.1 26.7 %collective-permute-start.14 = (bf16[352,1024]{1,0:T(8,128)(2,1)S(1)}, bf16[352,1024]{1,0:T(8,128)(2,1)S(1)}, u32[]{:S(2)}, u32[]{:S(2)}) collective-permute-start(bf16[352,1024]{1,0:T(8,128)(2,1)S(1)} %pad_maximum_fusion.2), channel_id=1, source_target_pairs={{0,128},{16,144},{32,160},{48,176},{64,192},{80,208},{96,224},{112... | collective-permute-start | bytes 2162696 | tf_op jit(solution)/shard_map/ppermute | solution.py:16
  168.3 43.2 %copy-start.4 = (bf16[352,1024]{1,0:T(8,128)(2,1)}, bf16[352,1024]{1,0:T(8,128)(2,1)S(1)}, u32[]{:S(2)}) copy-start(bf16[352,1024]{1,0:T(8,128)(2,1)S(1)} %pad_maximum_fusion.3) | copy-start | bytes 2162692
  168.3 30.4 %collective-permute-start.18 = (bf16[352,1024]{1,0:T(8,128)(2,1)S(1)}, bf16[352,1024]{1,0:T(8,128)(2,1)S(1)}, u32[]{:S(2)}, u32[]{:S(2)}) collective-permute-start(bf16[352,1024]{1,0:T(8,128)(2,1)S(1)} %pad_maximum_fusion.3), channel_id=1, source_target_pairs={{0,384},{16,400},{32,416},{48,432},{64,448},{80,464},{96,480},{112... | collective-permute-start | bytes 2162696 | tf_op jit(solution)/shard_map/ppermute | solution.py:16
  173.2 35.0 %collective-permute-start.15 = (bf16[352,1024]{1,0:T(8,128)(2,1)S(1)}, bf16[352,1024]{1,0:T(8,128)(2,1)S(1)}, u32[]{:S(2)}, u32[]{:S(2)}) collective-permute-start(bf16[352,1024]{1,0:T(8,128)(2,1)S(1)} %pad_maximum_fusion.3), channel_id=1, source_target_pairs={{0,128},{16,144},{32,160},{48,176},{64,192},{80,208},{96,224},{112... | collective-permute-start | bytes 2162696 | tf_op jit(solution)/shard_map/ppermute | solution.py:16
  177.3 24.6 %copy-start.7 = (bf16[352,1024]{1,0:T(8,128)(2,1)}, bf16[352,1024]{1,0:T(8,128)(2,1)S(1)}, u32[]{:S(2)}) copy-start(bf16[352,1024]{1,0:T(8,128)(2,1)S(1)} %collective-permute-done.13) | copy-start | bytes 2162692
  177.3 36.6 %collective-permute-start.22 = (bf16[176,1024]{1,0:T(8,128)(2,1)}, bf16[176,1024]{1,0:T(8,128)(2,1)S(1)}, u32[]{:S(2)}, u32[]{:S(2)}) collective-permute-start(bf16[176,1024]{1,0:T(8,128)(2,1)} %slice.95), channel_id=1, source_target_pairs={{0,384},{16,400},{32,416},{48,432},{64,448},{80,464},{96,480},{112... | collective-permute-start | bytes 1081352 | tf_op jit(solution)/shard_map/ppermute | solution.py:16
  183.3 28.3 %copy-start.9 = (bf16[352,1024]{1,0:T(8,128)(2,1)}, bf16[352,1024]{1,0:T(8,128)(2,1)S(1)}, u32[]{:S(2)}) copy-start(bf16[352,1024]{1,0:T(8,128)(2,1)S(1)} %collective-permute-done.17) | copy-start | bytes 2162692
  183.3 42.0 %collective-permute-start.19 = (bf16[176,1024]{1,0:T(8,128)(2,1)}, bf16[176,1024]{1,0:T(8,128)(2,1)}, u32[]{:S(2)}, u32[]{:S(2)}) collective-permute-start(bf16[176,1024]{1,0:T(8,128)(2,1)} %slice.92), channel_id=1, source_target_pairs={{0,128},{16,144},{32,160},{48,176},{64,192},{80,208},{96,224},{112... | collective-permute-start | bytes 1081352 | tf_op jit(solution)/shard_map/ppermute | solution.py:16
  192.8 18.8 %copy-start.8 = (bf16[352,1024]{1,0:T(8,128)(2,1)}, bf16[352,1024]{1,0:T(8,128)(2,1)S(1)}, u32[]{:S(2)}) copy-start(bf16[352,1024]{1,0:T(8,128)(2,1)S(1)} %collective-permute-done.14) | copy-start | bytes 2162692
  192.8 25.4 %collective-permute-start.23 = (bf16[176,1024]{1,0:T(8,128)(2,1)}, bf16[176,1024]{1,0:T(8,128)(2,1)}, u32[]{:S(2)}, u32[]{:S(2)}) collective-permute-start(bf16[176,1024]{1,0:T(8,128)(2,1)} %slice.96), channel_id=1, source_target_pairs={{0,384},{16,400},{32,416},{48,432},{64,448},{80,464},{96,480},{112... | collective-permute-start | bytes 1081352 | tf_op jit(solution)/shard_map/ppermute | solution.py:16
  198.7 12.8 %copy-start.11 = (bf16[352,1024]{1,0:T(8,128)(2,1)}, bf16[352,1024]{1,0:T(8,128)(2,1)S(1)}, u32[]{:S(2)}) copy-start(bf16[352,1024]{1,0:T(8,128)(2,1)S(1)} %collective-permute-done.18) | copy-start | bytes 2162692
  198.7 32.1 %collective-permute-start.20 = (bf16[176,1024]{1,0:T(8,128)(2,1)}, bf16[176,1024]{1,0:T(8,128)(2,1)}, u32[]{:S(2)}, u32[]{:S(2)}) collective-permute-start(bf16[176,1024]{1,0:T(8,128)(2,1)} %slice.93), channel_id=1, source_target_pairs={{0,128},{16,144},{32,160},{48,176},{64,192},{80,208},{96,224},{112... | collective-permute-start | bytes 1081352 | tf_op jit(solution)/shard_map/ppermute | solution.py:16
  208.2 3.4 %copy-start.10 = (bf16[352,1024]{1,0:T(8,128)(2,1)}, bf16[352,1024]{1,0:T(8,128)(2,1)S(1)}, u32[]{:S(2)}) copy-start(bf16[352,1024]{1,0:T(8,128)(2,1)S(1)} %collective-permute-done.15) | copy-start | bytes 2162692
  208.2 9.9 %collective-permute-start.24 = (bf16[176,1024]{1,0:T(8,128)(2,1)}, bf16[176,1024]{1,0:T(8,128)(2,1)}, u32[]{:S(2)}, u32[]{:S(2)}) collective-permute-start(bf16[176,1024]{1,0:T(8,128)(2,1)} %slice.97), channel_id=1, source_target_pairs={{0,384},{16,400},{32,416},{48,432},{64,448},{80,464},{96,480},{112... | collective-permute-start | bytes 1081352 | tf_op jit(solution)/shard_map/ppermute | solution.py:16
  213.9 16.9 %collective-permute-start.21 = (bf16[176,1024]{1,0:T(8,128)(2,1)}, bf16[176,1024]{1,0:T(8,128)(2,1)}, u32[]{:S(2)}, u32[]{:S(2)}) collective-permute-start(bf16[176,1024]{1,0:T(8,128)(2,1)} %slice.94), channel_id=1, source_target_pairs={{0,128},{16,144},{32,160},{48,176},{64,192},{80,208},{96,224},{112... | collective-permute-start | bytes 1081352 | tf_op jit(solution)/shard_map/ppermute | solution.py:16
  237.1 15.8 %copy-start.28 = (s32[2,8]{1,0:T(2,128)S(1)}, s32[2,8]{1,0:T(2,128)}, u32[]{:S(2)}) copy-start(s32[2,8]{1,0:T(2,128)} %param.24) | copy-start | bytes 196
  237.1 16.2 %copy-start.6 = (bf16[132,1024]{1,0:T(8,128)(2,1)S(1)}, bf16[132,1024]{1,0:T(8,128)(2,1)}, u32[]{:S(2)}) copy-start(bf16[132,1024]{1,0:T(8,128)(2,1)} %copy-done.5) | copy-start | bytes 811012
  239.4 60.6 %all-to-all-start.2 = ((bf16[16,21,1024]{2,1,0:T(8,128)(2,1)}), bf16[16,21,1024]{2,1,0:T(8,128)(2,1)S(1)}, u32[]{:S(2)}, u32[]{:S(2)}) async-start(bf16[16,21,1024]{2,1,0:T(8,128)(2,1)} %reshape.234), calls=%async_computation.2 | async-start | bytes 1572864 | tf_op jit(solution)/shard_map/all_to_all | solution.py:215
  253.5 47.2 %copy-start.2 = (f32[132,1024]{1,0:T(8,128)S(1)}, f32[132,1024]{1,0:T(8,128)}, u32[]{:S(2)}) copy-start(f32[132,1024]{1,0:T(8,128)} %copy-done.1) | copy-start | bytes 1622020
  300.8 2.0 copy-start.12

commit v2 on v0

--- a/solution.py
+++ b/solution.py
@@ -1,20 +1,271 @@
+import functools
+
 import jax
 import jax.numpy as jnp
 from jax import lax
+from jax.experimental import pallas as pl
+from jax.experimental.pallas import tpu as pltpu
 from jax.sharding import PartitionSpec as P
 
 HEADS = 8
 HD = 64
 
 
-def combined_all(part, axis, combine):
-    gathered = jax.tree.map(lambda a: lax.all_gather(a, axis), part)
-
-    def take(source):
-        return jax.tree.map(lambda a: lax.dynamic_index_in_dim(a, source, 0, False), gathered)
-
-    return lax.fori_loop(
-        1, lax.axis_size(axis), lambda source, state: combine(state, take(source)), take(0)
+LINE = 8
+RING = 4
+SLOT = 48
+
+
+def sends_of(condition, descriptor, started):
+    @pl.when(condition)
+    def _():
+        descriptor().start()
+
+    started.append((condition, descriptor))
+
+
+def remote(source, target, send_sem, recv_sem, device):
+    return pltpu.make_async_remote_copy(
+        src_ref=source,
+        dst_ref=target,
+        send_sem=send_sem,
+        recv_sem=recv_sem,
+        device_id=device,
+        device_id_type=pl.DeviceIdType.MESH,
+    )
+
+
+def signal(barrier, device):
+    pl.semaphore_signal(barrier, inc=1, device_id=device, device_id_type=pl.DeviceIdType.MESH)
+
+
+def gather_kernel(count, with_rows, *refs):
+    inputs = refs[:count]
+    refs = refs[count:]
+    if with_rows:
+        rows_in, refs = refs[0], refs[1:]
+    outputs = refs[:count]
+    refs = refs[count:]
+    if with_rows:
+        rows_out, refs = refs[0], refs[1:]
+    local_sem, recv_sem, up_sem, down_sem, right_sem, left_sem, far_sem = refs[:7]
+    if with_rows:
+        rows_local, rows_recv, rows_send = refs[7:]
+    blk = lax.axis_index("blk")
+    x = blk // LINE
+    z = blk % LINE
+    right = {"blk": ((x + 1) % RING) * LINE + z}
+    left = {"blk": ((x + RING - 1) % RING) * LINE + z}
+    above = {"blk": blk + 1}
+    below = {"blk": blk - 1}
+    has_up = z < LINE - 1
+    has_down = z > 0
+    started = []
+
+    barrier = pltpu.get_barrier_semaphore()
+    signal(barrier, right)
+    signal(barrier, left)
+
+    @pl.when(has_up)
+    def _():
+        signal(barrier, above)
+
+    @pl.when(has_down)
+    def _():
+        signal(barrier, below)
+
+    neighbours = 2 + has_up.astype(jnp.int32) + has_down.astype(jnp.int32)
+    if with_rows:
+        place = lax.axis_index("expert")
+        half = place // 8
+        y = (place // 2) % 4
+        core = place % 2
+
+        def at(h, row, c):
+            return (h % 2) * 8 + (row % 4) * 2 + c % 2
+
+        across = {"expert": at(half + 1, y, core)}
+        partner = {"expert": at(half, y, core + 1)}
+        ahead = {"expert": at(half, y + 1, core)}
+        behind = {"expert": at(half, y + 3, core)}
+        for device in (across, partner, ahead, behind):
+            signal(barrier, device)
+        neighbours = neighbours + 4
+    pl.semaphore_wait(barrier, neighbours)
+
+    def send(k, slot, source, sem, device):
+        return lambda: remote(source(), outputs[k].at[slot], sem, recv_sem.at[k, slot], device)
+
+    def arrive(k, slot):
+        piece = outputs[k].at[slot]
+        remote(piece, piece, far_sem.at[k, 0], recv_sem.at[k, slot], right).wait_recv()
+
+    def row_send(index, slot, source, device):
+        copy = remote(source, rows_out.at[slot], rows_send.at[index], rows_recv.at[slot], device)
+        copy.start()
+        row_started.append(copy)
+
+    def row_arrive(slot):
+        piece = rows_out.at[slot]
+        remote(piece, piece, rows_send.at[0], rows_recv.at[slot], across).wait_recv()
+
+    row_started = []
+    always = z >= 0
+    if with_rows:
+        row_send(0, place, rows_in, across)
+        own_rows = pltpu.make_async_copy(rows_in, rows_out.at[place], rows_local)
+        own_rows.start()
+
+    own_copies = []
+    for k in range(count):
+        own = lambda k=k: inputs[k]
+        sends_of(has_up, send(k, blk, own, up_sem.at[k, 0], above), started)
+        sends_of(has_down, send(k, blk, own, down_sem.at[k, 0], below), started)
+        sends_of(always, send(k, blk, own, right_sem.at[k, 0], right), started)
+        sends_of(always, send(k, blk, own, left_sem.at[k, 0], left), started)
+        copy = pltpu.make_async_copy(inputs[k], outputs[k].at[blk], local_sem.at[k])
+        copy.start()
+        own_copies.append(copy)
+
+    for distance in range(1, LINE):
+        for direction in (0, 1):
+            slot = blk - distance if direction == 0 else blk + distance
+            present = z >= distance if direction == 0 else z + distance < LINE
+            onward = has_up if direction == 0 else has_down
+            target = above if direction == 0 else below
+            z_sem = up_sem if direction == 0 else down_sem
+            index = distance + direction * LINE
+            for k in range(count):
+                held = lambda k=k, slot=slot: outputs[k].at[slot]
+
+                @pl.when(present)
+                def _(k=k, slot=slot):
+                    arrive(k, slot)
+
+                sends_of(
+                    jnp.logical_and(present, onward),
+                    send(k, slot, held, z_sem.at[k, distance], target),
+                    started,
+                )
+                sends_of(present, send(k, slot, held, right_sem.at[k, index], right), started)
+                sends_of(present, send(k, slot, held, left_sem.at[k, index], left), started)
+        if with_rows and distance == 2:
+            row_arrive(at(half + 1, y, core))
+            for h in range(2):
+                slot = at(half + h, y, core)
+                source = rows_in if h == 0 else rows_out.at[slot]
+                row_send(1 + h, slot, source, partner)
+        if with_rows and distance == 3:
+            for h in range(2):
+                row_arrive(at(half + h, y, core + 1))
+            for h in range(2):
+                for c in range(2):
+                    slot = at(half + h, y, core + c)
+                    source = rows_in if h + c == 0 else rows_out.at[slot]
+                    row_send(3 + 2 * h + c, slot, source, ahead)
+                    row_send(7 + 2 * h + c, slot, source, behind)
+        if with_rows and distance == 6:
+            for c in range(2):
+                for h in range(2):
+                    row_arrive(at(h, y + 3, c))
+                    row_arrive(at(h, y + 1, c))
+                slot = at(0, y + 3, c)
+                row_send(11 + c, slot, rows_out.at[slot], ahead)
+                slot = at(1, y + 1, c)
+                row_send(13 + c, slot, rows_out.at[slot], behind)
+
+    before = ((x + RING - 1) % RING) * LINE
+    after = ((x + 1) % RING) * LINE
+    opposite = ((x + 2) % RING) * LINE
+    for order in range(LINE):
+        for k in range(count):
+            line = (z + order) % LINE
+            from_left, from_right = before + line, after + line
+            arrive(k, from_left)
+            arrive(k, from_right)
+            sem = far_sem.at[k, order]
+            even = line % 2 == 0
+            first = lambda k=k, slot=from_left: outputs[k].at[slot]
+            second = lambda k=k, slot=from_right: outputs[k].at[slot]
+            sends_of(even, send(k, from_left, first, sem, right), started)
+            sends_of(jnp.logical_not(even), send(k, from_right, second, sem, left), started)
+    for line in range(LINE):
+        for k in range(count):
+            arrive(k, opposite + line)
+    if with_rows:
+        for h in range(2):
+            for c in range(2):
+                row_arrive(at(h, y + 2, c))
+        for copy in row_started:
+            copy.wait_send()
+        own_rows.wait()
+    for copy in own_copies:
+        copy.wait()
+    for condition, descriptor in started:
+
+        @pl.when(condition)
+        def _(descriptor=descriptor):
+            descriptor().wait_send()
+
+
+def gather_blocks(blocks, rows, collective_id):
+    count = len(blocks)
+    with_rows = rows is not None
+    blocks = [jnp.pad(block, ((0, SLOT - block.shape[0]), (0, 0))) for block in blocks]
+    width = blocks[0].shape[1]
+    dma = pltpu.SemaphoreType.DMA
+    shapes = [jax.ShapeDtypeStruct((RING * LINE, SLOT, width), jnp.bfloat16)] * count
+    operands = list(blocks)
+    scratch = [
+        dma((count,)),
+        dma((count, RING * LINE)),
+        dma((count, LINE)),
+        dma((count, LINE)),
+        dma((count, 2 * LINE)),
+        dma((count, 2 * LINE)),
+        dma((count, LINE)),
+    ]
+    if with_rows:
+        operands.append(rows)
+        shapes.append(jax.ShapeDtypeStruct((16,) + rows.shape, jnp.bfloat16))
+        scratch += [dma(()), dma((16,)), dma((15,))]
+    gathered = pl.pallas_call(
+        functools.partial(gather_kernel, count, with_rows),
+        out_shape=shapes,
+        in_specs=[pl.BlockSpec(memory_space=pltpu.VMEM)] * len(operands),
+        out_specs=[pl.BlockSpec(memory_space=pl.ANY)] * len(shapes),
+        scratch_shapes=scratch,
+        compiler_params=pltpu.CompilerParams(collective_id=collective_id, has_side_effects=True),
+        cost_estimate=pl.CostEstimate(
+            flops=0, bytes_accessed=100_000_000 * count, transcendentals=0
+        ),
+    )(*operands)
+    return [array.reshape(-1, array.shape[-1]) for array in gathered]
+
+
+def scatter_parts(part, share_rows):
+    peaks, totals, output = part
+    count, tree = peaks.shape[:2]
+    packed = jnp.concatenate([output, peaks, totals], axis=-1)
+    width = packed.shape[-1]
+    packed = packed.reshape(count, tree // share_rows, share_rows, width).transpose(1, 0, 2, 3)
+    arrived = lax.all_to_all(packed, "blk", split_axis=0, concat_axis=0, tiled=True)
+    wide = output.shape[-1]
+    return (
+        arrived[..., wide : wide + HEADS],
+        arrived[..., wide + HEADS :],
+        arrived[..., :wide],
+    )
+
+
+def join_many(parts):
+    peaks, totals, output = parts
+    highest = jnp.max(peaks, axis=0)
+    scale = jnp.exp(peaks - highest[None])
+    return (
+        highest,
+        jnp.sum(scale * totals, axis=0),
+        jnp.sum(expand(scale, output), axis=0),
     )
 
 
@@ -102,10 +353,8 @@
     local_part = block_part(long_queries, heads_of(long_keys), heads_of(long_values), everything)
     share_rows = tree_size // lax.axis_size("blk")
     share_start = lax.axis_index("blk") * share_rows
-    merged = combined_all(local_part, "blk", pair_join)
-    cache_part = tuple(
-        (lax.dynamic_slice_in_dim(member, share_start, share_rows, 1) for member in merged)
-    )
+    down_weight, projection = gather_blocks([expert_out[0]], out_weight, 0)
+    cache_part = join_many(scatter_parts(local_part, share_rows))
     share_queries = lax.dynamic_slice_in_dim(long_queries, share_start, share_rows, 1)
     share_mask = lax.dynamic_slice_in_dim(long_mask, share_start, share_rows, 1)
     long_tree = block_part(
@@ -120,7 +369,7 @@
     row_count = attn_rows.shape[0]
     projected = jnp.dot(
         attn_rows,
-        lax.all_gather(out_weight, "expert", axis=0, tiled=True),
+        projection,
         preferred_element_type=jnp.float32,
     )
     layer_state = (residual.astype(jnp.float32) + projected).astype(jnp.bfloat16)
@@ -145,19 +394,15 @@
     dispatch = jnp.dot(
         placement, jnp.repeat(normed, 2, axis=0), preferred_element_type=jnp.float32
     ).astype(jnp.bfloat16)
+    dispatch, own_in = lax.optimization_barrier((dispatch, expert_in))
     dispatch = dispatch.reshape(expert_count, capacity, model_width)
     received = lax.all_to_all(dispatch, "expert", split_axis=0, concat_axis=0, tiled=True)
     flat_rows = received.reshape(-1, model_width)
-    weight_in = lax.all_gather(expert_in, "blk", axis=1, tiled=True)[0]
-    weight_out = lax.all_gather(expert_out, "blk", axis=1, tiled=True)[0]
-    gate_part = jnp.einsum(
-        "rd,nd->rn", flat_rows, weight_in[:, 0, :], preferred_element_type=jnp.float32
-    )
-    up_part = jnp.einsum(
-        "rd,nd->rn", flat_rows, weight_in[:, 1, :], preferred_element_type=jnp.float32
-    )
+    gate_weight, up_weight = gather_blocks([own_in[0, :, 0, :], own_in[0, :, 1, :]], None, 1)
+    gate_part = jnp.einsum("rd,nd->rn", flat_rows, gate_weight, preferred_element_type=jnp.float32)
+    up_part = jnp.einsum("rd,nd->rn", flat_rows, up_weight, preferred_element_type=jnp.float32)
     inner_act = (jax.nn.gelu(gate_part, approximate=True) * up_part).astype(jnp.bfloat16)
-    expert_sum = jnp.dot(inner_act, weight_out, preferred_element_type=jnp.float32)
+    expert_sum = jnp.dot(inner_act, down_weight, preferred_element_type=jnp.float32)
     expert_y = expert_sum.astype(jnp.bfloat16).reshape(expert_count, capacity, model_width)
     returned = lax.all_to_all(expert_y, "expert", split_axis=0, concat_axis=0, tiled=True)
     per_route = jnp.einsum(

time: 907 us -> 252 us (0.28)
  the two profiles are of different devices: /device:TPU:1 before, /device:TPU:32 now
where the time goes in v2:
time: 252 us; the launch traced here: 251 us
  Pallas kernels  139 us (55%)
  waiting for transfers between devices  47.1 us (19%)
  starting transfers between devices  30.3 us (12%)
  matrix products  14.7 us (6%)
  local copies, waits for them, and re-layouts  14.1 us (6%)
  other arithmetic  4.65 us (2%)
    pallas_call x2, Pallas kernels, gather_blocks(): pl.pallas_call(functools.partial(gather_kernel, count, with_rows), out_sh...  139 us
    all_to_all x1, waiting for transfers between devices, on_device(): lax.all_to_all(expert_y, 'expert', split_axis=0, concat_axis=0, tiled=True)  47.1 us
    all_to_all x1, starting transfers between devices, scatter_parts(): lax.all_to_all(packed, 'blk', split_axis=0, concat_axis=0, tiled=True)  15.2 us
    all_to_all x1, starting transfers between devices, on_device(): lax.all_to_all(dispatch, 'expert', split_axis=0, concat_axis=0, tiled=True)  9.69 us
    dot_general x1, matrix products, on_device(): jnp.dot(inner_act, down_weight, preferred_element_type=jnp.float32)  5.93 us
    all_to_all x1, starting transfers between devices, on_device(): lax.all_to_all(expert_y, 'expert', split_axis=0, concat_axis=0, tiled=True)  5.39 us
  transfers between devices with their start and end apart: 3, of which 1 were waited for; matrix products, arithmetic and copies ran while one was open for 4% of the time, Pallas kernels for 55%

profile of v2, /device:TPU:32, one launch (start us, length us, event | category | flops | bytes accessed | tf_op | source)
XLA Modules:
  0.0 251.0 jit_solution(4304199365277987535)
XLA Ops:
  0.6 1.1 fusion.62
  1.7 0.2 reshape_squeeze.21
  1.9 1.3 copy.212
  3.2 0.4 fusion.64
  3.7 0.4 convert_reduce_fusion
  4.2 0.2 copy.214
  4.4 0.4 convolution_bitcast_fusion.2
  4.8 0.3 copy.215
  5.2 0.2 concatenate.17
  5.4 0.2 maximum_bitcast_fusion
  5.6 0.8 copy.218
  6.4 15.2 %all-to-all-start = ((f32[32,2,2,528]{3,2,1,0:T(2,128)}), f32[32,2,2,528]{3,2,1,0:T(2,128)S(1)}, u32[]{:S(2)}, u32[]{:S(2)}) async-start(f32[32,2,2,528]{3,2,1,0:T(2,128)} %copy.218), calls=%async_computation | async-start | bytes 655360 | tf_op jit(solution)/shard_map/all_to_all | solution.py:252
  22.0 0.1 reshape.237
  22.2 0.9 reduce-window.6
  23.1 0.2 slice_reduce_fusion.1
  23.3 0.2 copy.203
  23.5 0.2 copy.205
  23.8 0.2 reshape_squeeze.18
  24.0 0.2 reshape_squeeze.20
  24.1 0.2 reshape_squeeze.19
  24.3 0.3 fusion.65
  24.6 0.4 fusion.66
  25.0 0.4 convert_reduce_fusion.2
  25.4 0.1 convert_reduce_fusion.1
  25.5 0.3 fusion.13
  25.9 0.5 fusion.20
  26.4 0.2 copy.211
  26.5 0.2 convert_element_type.80
  26.8 0.2 reshape_squeeze.23
  26.9 0.2 reshape_squeeze.22
  27.1 0.7 dynamic-slice_compare_fusion
  27.9 0.3 fusion.63
  28.3 0.2 convert_reduce_fusion.3
  28.5 0.7 pad.14.refs_0_
  29.2 51.7 %shard_map.193 = (bf16[32,48,1024]{2,1,0:T(8,128)(2,1)}, bf16[16,32,1024]{2,1,0:T(8,128)(2,1)}) custom-call(bf16[48,1024]{1,0:T(8,128)(2,1)} %pad.14.refs_0_, bf16[32,1024]{1,0:T(8,128)(2,1)} %refs_1_.1), custom_call_target="tpu_custom_call" | custom-call | bytes 100000000 | tf_op jit(solution)/shard_map/pallas_call | solution.py:232
  81.0 0.2 fusion.28
  81.3 0.1 fusion.39
  81.4 0.2 mul.189
  81.6 0.2 mul.190
  81.8 0.2 fusion.27
  82.3 0.4 multiply_reduce_fusion
  82.7 0.1 multiply_convert_fusion
  82.9 0.3 broadcast_in_dim.98
  83.2 0.2 reshape.240
  83.4 0.5 convolution_convert_fusion.1
  83.9 1.1 reshape.241
  85.0 9.7 %all-to-all-start.1 = ((bf16[16,21,1024]{2,1,0:T(8,128)(2,1)}), bf16[16,21,1024]{2,1,0:T(8,128)(2,1)S(1)}, u32[]{:S(2)}, u32[]{:S(2)}) async-start(bf16[16,21,1024]{2,1,0:T(8,128)(2,1)} %reshape.241), calls=%async_computation.1 | async-start | bytes 1572864 | tf_op jit(solution)/shard_map/all_to_all | solution.py:399
  94.8 0.7 pad.17.refs_1_
  95.5 0.6 pad.16.refs_0_
  96.1 87.2 %shard_map.194 = (bf16[32,48,1024]{2,1,0:T(8,128)(2,1)}, bf16[32,48,1024]{2,1,0:T(8,128)(2,1)}) custom-call(bf16[48,1024]{1,0:T(8,128)(2,1)} %pad.16.refs_0_, bf16[48,1024]{1,0:T(8,128)(2,1)} %pad.17.refs_1_), custom_call_target="tpu_custom_call" | custom-call | bytes 200000000 | tf_op jit(solution)/shard_map/pallas_call | solution.py:232
  183.3 0.2 reshape.242
  183.5 4.5 %fusion.67 = f32[336,1536]{1,0:T(8,128)} fusion(bf16[336,1024]{1,0:T(8,128)(2,1)S(1)} %reshape.242, bf16[1536,1024]{1,0:T(8,128)(2,1)} %bitcast.129), kind=kOutput, calls=%fused_computation.124 | convolution fusion | flops 1056964608 | bytes 5898240 | tf_op jit(solution)/shard_map/rd,nd->rn/dot_general | solution.py:402
  188.0 5.9 %convolution_convert_fusion = bf16[336,1024]{1,0:T(8,128)(2,1)S(1)} fusion(bf16[1536,1024]{1,0:T(8,128)(2,1)} %bitcast.127, bf16[336,1024]{1,0:T(8,128)(2,1)S(1)} %reshape.242, bf16[1536,1024]{1,0:T(8,128)(2,1)} %bitcast.128, f32[336,1536]{1,0:T(8,128)} %fusion.67), kind=kOutput, calls=%fused_computation.14 | convolution fusion | flops 2119434240 | bytes 9732096 | tf_op jit(solution)/shard_map/dot_general | solution.py:405
  193.9 1.1 reshape.246
  195.0 5.4 %all-to-all-start.2 = ((bf16[16,21,1024]{2,1,0:T(8,128)(2,1)}), bf16[16,21,1024]{2,1,0:T(8,128)(2,1)S(1)}, u32[]{:S(2)}, u32[]{:S(2)}) async-start(bf16[16,21,1024]{2,1,0:T(8,128)(2,1)} %reshape.246), calls=%async_computation.2 | async-start | bytes 1572864 | tf_op jit(solution)/shard_map/all_to_all | solution.py:407
  200.5 0.1 iota_compare_fusion.2
  200.7 0.1 eq.80
  200.8 0.2 fusion.23
  201.1 47.1 %all-to-all-done.2 = bf16[16,21,1024]{2,1,0:T(8,128)(2,1)S(1)} async-done(((bf16[16,21,1024]{2,1,0:T(8,128)(2,1)}), bf16[16,21,1024]{2,1,0:T(8,128)(2,1)S(1)}, u32[]{:S(2)}, u32[]{:S(2)}) %all-to-all-start.2) | async-done | bytes 688160 | tf_op jit(solution)/shard_map/all_to_all | solution.py:407
  248.1 0.2 reshape.262
  248.4 0.5 fusion.9
  249.0 0.7 reshape.249
  249.6 0.7 gather_fusion
  250.3 0.7 bitcast_select_fusion
  (68 shorter events, 1.6 us)
Async XLA Ops:
  0.6 200.2 %copy-start = (bf16[1024,16]{0,1:T(8,128)(2,1)S(1)}, bf16[1024,16]{0,1:T(8,128)(2,1)}, u32[]{:S(2)}) copy-start(bf16[1024,16]{0,1:T(8,128)(2,1)} %param.32) | copy-start | bytes 98308
  1.9 2.3 copy-start.3
  4.8 16.9 %copy-start.15 = (s32[2]{0:T(128)S(1)}, s32[2]{0:T(128)}, u32[]{:S(2)}) copy-start(s32[2]{0:T(128)} %param.22) | copy-start | bytes 28
  4.8 17.0 %copy-start.13 = (bf16[1024]{0:T(1024)(128)(2,1)S(1)}, bf16[1024]{0:T(1024)(128)(2,1)}, u32[]{:S(2)}) copy-start(bf16[1024]{0:T(1024)(128)(2,1)} %param.31) | copy-start | bytes 6148
  4.8 17.0 %copy-start.12 = (bf16[2,2,1024]{2,1,0:T(2,128)(2,1)S(1)}, bf16[2,2,1024]{2,1,0:T(2,128)(2,1)}, u32[]{:S(2)}) copy-start(bf16[2,2,1024]{2,1,0:T(2,128)(2,1)} %param.29) | copy-start | bytes 24580
  4.8 17.0 %copy-start.10 = (s32[2,64,64]{2,1,0:T(8,128)S(1)}, s32[2,64,64]{2,1,0:T(8,128)}, u32[]{:S(2)}) copy-start(s32[2,64,64]{2,1,0:T(8,128)} %param.19) | copy-start | bytes 98308
  4.8 17.1 %copy-start.11 = (s32[132,2]{0,1:T(2,128)S(1)}, s32[132,2]{0,1:T(2,128)}, u32[]{:S(2)}) copy-start(s32[132,2]{0,1:T(2,128)} %param.33) | copy-start | bytes 3172
  5.1 18.2 %copy-start.6 = (bf16[2,128,512]{2,1,0:T(8,128)(2,1)S(1)}, bf16[2,128,512]{2,1,0:T(8,128)(2,1)}, u32[]{:S(2)}) copy-start(bf16[2,128,512]{2,1,0:T(8,128)(2,1)} %param.20) | copy-start | bytes 786436
  5.2 18.4 %copy-start.7 = (bf16[2,128,512]{2,1,0:T(8,128)(2,1)S(1)}, bf16[2,128,512]{2,1,0:T(8,128)(2,1)}, u32[]{:S(2)}) copy-start(bf16[2,128,512]{2,1,0:T(8,128)(2,1)} %param.21) | copy-start | bytes 786436
  5.4 18.3 %copy-start.4 = (bf16[2,64,3,512]{3,1,2,0:T(8,128)(2,1)S(1)}, bf16[2,64,3,512]{3,1,2,0:T(8,128)(2,1)}, u32[]{:S(2)}) copy-start(bf16[2,64,3,512]{3,1,2,0:T(8,128)(2,1)} %param.18) | copy-start | bytes 1179652
  6.4 74.9 %all-to-all-start = ((f32[32,2,2,528]{3,2,1,0:T(2,128)}), f32[32,2,2,528]{3,2,1,0:T(2,128)S(1)}, u32[]{:S(2)}, u32[]{:S(2)}) async-start(f32[32,2,2,528]{3,2,1,0:T(2,128)} %copy.218), calls=%async_computation | async-start | bytes 655360 | tf_op jit(solution)/shard_map/all_to_all | solution.py:252
  25.8 2.7 %copy-start.9 = (bf16[1,44,1024]{2,1,0:T(8,128)(2,1)S(1)}, bf16[1,44,1024]{2,1,0:T(8,128)(2,1)}, u32[]{:S(2)}) copy-start(bf16[1,44,1024]{2,1,0:T(8,128)(2,1)} %param.35) | copy-start | bytes 270340
  26.7 55.5 %copy-start.5 = (bf16[128,1024]{1,0:T(8,128)(2,1)S(1)}, bf16[128,1024]{1,0:T(8,128)(2,1)}, u32[]{:S(2)}) copy-start(bf16[128,1024]{1,0:T(8,128)(2,1)} %param.23) | copy-start | bytes 786436
  80.9 1.4 copy-start.1
  83.4 11.4 %copy-start.8 = (bf16[1,44,2,1024]{3,2,1,0:T(2,128)(2,1)S(1)}, bf16[1,44,2,1024]{3,2,1,0:T(2,128)(2,1)}, u32[]{:S(2)}) copy-start(bf16[1,44,2,1024]{3,2,1,0:T(2,128)(2,1)} %param.34) | copy-start | bytes 540676
  85.0 98.3 %all-to-all-start.1 = ((bf16[16,21,1024]{2,1,0:T(8,128)(2,1)}), bf16[16,21,1024]{2,1,0:T(8,128)(2,1)S(1)}, u32[]{:S(2)}, u32[]{:S(2)}) async-start(bf16[16,21,1024]{2,1,0:T(8,128)(2,1)} %reshape.241), calls=%async_computation.1 | async-start | bytes 1572864 | tf_op jit(solution)/shard_map/all_to_all | solution.py:399
  193.9 6.5 %copy-start.14 = (s32[2,8]{1,0:T(2,128)S(1)}, s32[2,8]{1,0:T(2,128)}, u32[]{:S(2)}) copy-start(s32[2,8]{1,0:T(2,128)} %param.24) | copy-start | bytes 196
  195.0 53.1 %all-to-all-start.2 = ((bf16[16,21,1024]{2,1,0:T(8,128)(2,1)}), bf16[16,21,1024]{2,1,0:T(8,128)(2,1)S(1)}, u32[]{:S(2)}, u32[]{:S(2)}) async-start(bf16[16,21,1024]{2,1,0:T(8,128)(2,1)} %reshape.246), calls=%async_computation.2 | async-start | bytes 1572864 | tf_op jit(solution)/shard_map/all_to_all | solution.py:407
  249.0 2.0 copy-start.2

commit v3 on v2

--- a/solution.py
+++ b/solution.py
@@ -1,5 +1,4 @@
 import functools
-
 import jax
 import jax.numpy as jnp
 from jax import lax
@@ -127,6 +126,37 @@
         copy.start()
         own_copies.append(copy)
 
+    before = ((x + RING - 1) % RING) * LINE
+    after = ((x + 1) % RING) * LINE
+    opposite = ((x + 2) % RING) * LINE
+
+    def pass_on(distance):
+        for direction in (0, 1) if distance else (0,):
+            line = z - distance if direction == 0 else z + distance
+            present = z >= distance if direction == 0 else z + distance < LINE
+            even = line % 2 == 0
+            from_left, from_right = before + line, after + line
+            for k in range(count):
+
+                @pl.when(present)
+                def _(k=k, from_left=from_left, from_right=from_right):
+                    arrive(k, from_left)
+                    arrive(k, from_right)
+
+                sem = far_sem.at[k, distance + direction * LINE]
+                first = lambda k=k, slot=from_left: outputs[k].at[slot]
+                second = lambda k=k, slot=from_right: outputs[k].at[slot]
+                sends_of(
+                    jnp.logical_and(present, even),
+                    send(k, from_left, first, sem, right),
+                    started,
+                )
+                sends_of(
+                    jnp.logical_and(present, jnp.logical_not(even)),
+                    send(k, from_right, second, sem, left),
+                    started,
+                )
+
     for distance in range(1, LINE):
         for direction in (0, 1):
             slot = blk - distance if direction == 0 else blk + distance
@@ -149,6 +179,8 @@
                 )
                 sends_of(present, send(k, slot, held, right_sem.at[k, index], right), started)
                 sends_of(present, send(k, slot, held, left_sem.at[k, index], left), started)
+        if distance in (2, 4, 6):
+            pass_on(distance // 2 - 1)
         if with_rows and distance == 2:
             row_arrive(at(half + 1, y, core))
             for h in range(2):
@@ -174,21 +206,8 @@
                 slot = at(1, y + 1, c)
                 row_send(13 + c, slot, rows_out.at[slot], behind)
 
-    before = ((x + RING - 1) % RING) * LINE
-    after = ((x + 1) % RING) * LINE
-    opposite = ((x + 2) % RING) * LINE
-    for order in range(LINE):
-        for k in range(count):
-            line = (z + order) % LINE
-            from_left, from_right = before + line, after + line
-            arrive(k, from_left)
-            arrive(k, from_right)
-            sem = far_sem.at[k, order]
-            even = line % 2 == 0
-            first = lambda k=k, slot=from_left: outputs[k].at[slot]
-            second = lambda k=k, slot=from_right: outputs[k].at[slot]
-            sends_of(even, send(k, from_left, first, sem, right), started)
-            sends_of(jnp.logical_not(even), send(k, from_right, second, sem, left), started)
+    for distance in range(3, LINE):
+        pass_on(distance)
     for line in range(LINE):
         for k in range(count):
             arrive(k, opposite + line)
@@ -223,7 +242,7 @@
         dma((count, LINE)),
         dma((count, 2 * LINE)),
         dma((count, 2 * LINE)),
-        dma((count, LINE)),
+        dma((count, 2 * LINE)),
     ]
     if with_rows:
         operands.append(rows)

time: 252 us -> 252 us (level)
  transfers between devices with their start and end apart: 3 -> 3, of which waited for: 1 -> 1; matrix products, arithmetic and copies ran while one was open for 4% -> 4% of each run, Pallas kernels for 55% -> 56%
where the time goes in v3:
time: 252 us; the launch traced here: 251 us
  Pallas kernels  140 us (56%)
  waiting for transfers between devices  47.1 us (19%)
  starting transfers between devices  29.4 us (12%)
  matrix products  14.7 us (6%)
  local copies, waits for them, and re-layouts  14.1 us (6%)
  other arithmetic  4.65 us (2%)
    pallas_call x2, Pallas kernels, gather_blocks(): pl.pallas_call(functools.partial(gather_kernel, count, with_rows), out_sh...  140 us
    all_to_all x1, waiting for transfers between devices, on_device(): lax.all_to_all(expert_y, 'expert', split_axis=0, concat_axis=0, tiled=True)  47.1 us
    all_to_all x1, starting transfers between devices, scatter_parts(): lax.all_to_all(packed, 'blk', split_axis=0, concat_axis=0, tiled=True)  15.2 us
    all_to_all x1, starting transfers between devices, on_device(): lax.all_to_all(dispatch, 'expert', split_axis=0, concat_axis=0, tiled=True)  9.06 us
    dot_general x1, matrix products, on_device(): jnp.dot(inner_act, down_weight, preferred_element_type=jnp.float32)  5.92 us
    all_to_all x1, starting transfers between devices, on_device(): lax.all_to_all(expert_y, 'expert', split_axis=0, concat_axis=0, tiled=True)  5.11 us
  transfers between devices with their start and end apart: 3, of which 1 were waited for; matrix products, arithmetic and copies ran while one was open for 4% of the time, Pallas kernels for 56%

profile of v3, /device:TPU:32, one launch (start us, length us, event | category | flops | bytes accessed | tf_op | source)
XLA Modules:
  0.0 251.1 jit_solution(10155712747085225274)
XLA Ops:
  0.6 1.1 fusion.62
  1.7 0.2 reshape_squeeze.21
  1.9 1.3 copy.212
  3.2 0.4 fusion.64
  3.7 0.4 convert_reduce_fusion
  4.2 0.2 copy.214
  4.4 0.4 convolution_bitcast_fusion.2
  4.8 0.3 copy.215
  5.2 0.2 concatenate.17
  5.4 0.2 maximum_bitcast_fusion
  5.6 0.8 copy.218
  6.4 15.2 %all-to-all-start = ((f32[32,2,2,528]{3,2,1,0:T(2,128)}), f32[32,2,2,528]{3,2,1,0:T(2,128)S(1)}, u32[]{:S(2)}, u32[]{:S(2)}) async-start(f32[32,2,2,528]{3,2,1,0:T(2,128)} %copy.218), calls=%async_computation | async-start | bytes 655360 | tf_op jit(solution)/shard_map/all_to_all | solution.py:271
  22.0 0.1 reshape.237
  22.2 0.9 reduce-window.6
  23.1 0.2 slice_reduce_fusion.1
  23.3 0.2 copy.203
  23.5 0.2 copy.205
  23.8 0.2 reshape_squeeze.18
  24.0 0.2 reshape_squeeze.20
  24.1 0.2 reshape_squeeze.19
  24.3 0.3 fusion.65
  24.6 0.4 fusion.66
  25.0 0.4 convert_reduce_fusion.2
  25.4 0.1 convert_reduce_fusion.1
  25.5 0.3 fusion.13
  25.9 0.5 fusion.20
  26.4 0.2 copy.211
  26.5 0.2 convert_element_type.80
  26.8 0.2 reshape_squeeze.23
  26.9 0.2 reshape_squeeze.22
  27.1 0.7 dynamic-slice_compare_fusion
  27.9 0.3 fusion.63
  28.3 0.2 convert_reduce_fusion.3
  28.5 0.7 pad.14.refs_0_
  29.2 49.8 %shard_map.193 = (bf16[32,48,1024]{2,1,0:T(8,128)(2,1)}, bf16[16,32,1024]{2,1,0:T(8,128)(2,1)}) custom-call(bf16[48,1024]{1,0:T(8,128)(2,1)} %pad.14.refs_0_, bf16[32,1024]{1,0:T(8,128)(2,1)} %refs_1_.1), custom_call_target="tpu_custom_call" | custom-call | bytes 100000000 | tf_op jit(solution)/shard_map/pallas_call | solution.py:251
  79.2 0.2 fusion.28
  79.5 0.1 fusion.39
  79.6 0.2 mul.189
  79.8 0.2 mul.190
  80.0 0.2 fusion.27
  80.5 0.4 multiply_reduce_fusion
  80.9 0.1 multiply_convert_fusion
  81.1 0.3 broadcast_in_dim.98
  81.3 0.2 reshape.240
  81.6 0.5 convolution_convert_fusion.1
  82.1 1.1 reshape.241
  83.2 9.1 %all-to-all-start.1 = ((bf16[16,21,1024]{2,1,0:T(8,128)(2,1)}), bf16[16,21,1024]{2,1,0:T(8,128)(2,1)S(1)}, u32[]{:S(2)}, u32[]{:S(2)}) async-start(bf16[16,21,1024]{2,1,0:T(8,128)(2,1)} %reshape.241), calls=%async_computation.1 | async-start | bytes 1572864 | tf_op jit(solution)/shard_map/all_to_all | solution.py:418
  92.4 0.7 pad.17.refs_1_
  93.0 0.6 pad.16.refs_0_
  93.7 89.9 %shard_map.194 = (bf16[32,48,1024]{2,1,0:T(8,128)(2,1)}, bf16[32,48,1024]{2,1,0:T(8,128)(2,1)}) custom-call(bf16[48,1024]{1,0:T(8,128)(2,1)} %pad.16.refs_0_, bf16[48,1024]{1,0:T(8,128)(2,1)} %pad.17.refs_1_), custom_call_target="tpu_custom_call" | custom-call | bytes 200000000 | tf_op jit(solution)/shard_map/pallas_call | solution.py:251
  183.6 0.2 reshape.242
  183.9 4.5 %fusion.67 = f32[336,1536]{1,0:T(8,128)} fusion(bf16[336,1024]{1,0:T(8,128)(2,1)S(1)} %reshape.242, bf16[1536,1024]{1,0:T(8,128)(2,1)} %bitcast.129), kind=kOutput, calls=%fused_computation.124 | convolution fusion | flops 1056964608 | bytes 5898240 | tf_op jit(solution)/shard_map/rd,nd->rn/dot_general | solution.py:421
  188.3 5.9 %convolution_convert_fusion = bf16[336,1024]{1,0:T(8,128)(2,1)S(1)} fusion(bf16[1536,1024]{1,0:T(8,128)(2,1)} %bitcast.127, bf16[336,1024]{1,0:T(8,128)(2,1)S(1)} %reshape.242, bf16[1536,1024]{1,0:T(8,128)(2,1)} %bitcast.128, f32[336,1536]{1,0:T(8,128)} %fusion.67), kind=kOutput, calls=%fused_computation.14 | convolution fusion | flops 2119434240 | bytes 9732096 | tf_op jit(solution)/shard_map/dot_general | solution.py:424
  194.3 1.1 reshape.246
  195.4 5.1 %all-to-all-start.2 = ((bf16[16,21,1024]{2,1,0:T(8,128)(2,1)}), bf16[16,21,1024]{2,1,0:T(8,128)(2,1)S(1)}, u32[]{:S(2)}, u32[]{:S(2)}) async-start(bf16[16,21,1024]{2,1,0:T(8,128)(2,1)} %reshape.246), calls=%async_computation.2 | async-start | bytes 1572864 | tf_op jit(solution)/shard_map/all_to_all | solution.py:426
  200.6 0.1 iota_compare_fusion.2
  200.7 0.1 eq.80
  200.9 0.2 fusion.23
  201.1 47.1 %all-to-all-done.2 = bf16[16,21,1024]{2,1,0:T(8,128)(2,1)S(1)} async-done(((bf16[16,21,1024]{2,1,0:T(8,128)(2,1)}), bf16[16,21,1024]{2,1,0:T(8,128)(2,1)S(1)}, u32[]{:S(2)}, u32[]{:S(2)}) %all-to-all-start.2) | async-done | bytes 688160 | tf_op jit(solution)/shard_map/all_to_all | solution.py:426
  248.2 0.2 reshape.262
  248.4 0.5 fusion.9
  249.0 0.7 reshape.249
  249.7 0.7 gather_fusion
  250.4 0.7 bitcast_select_fusion
  (68 shorter events, 1.6 us)
Async XLA Ops:
  0.6 200.3 %copy-start = (bf16[1024,16]{0,1:T(8,128)(2,1)S(1)}, bf16[1024,16]{0,1:T(8,128)(2,1)}, u32[]{:S(2)}) copy-start(bf16[1024,16]{0,1:T(8,128)(2,1)} %param.32) | copy-start | bytes 98308
  1.9 2.3 copy-start.3
  4.8 16.9 %copy-start.15 = (s32[2]{0:T(128)S(1)}, s32[2]{0:T(128)}, u32[]{:S(2)}) copy-start(s32[2]{0:T(128)} %param.22) | copy-start | bytes 28
  4.8 17.0 %copy-start.13 = (bf16[1024]{0:T(1024)(128)(2,1)S(1)}, bf16[1024]{0:T(1024)(128)(2,1)}, u32[]{:S(2)}) copy-start(bf16[1024]{0:T(1024)(128)(2,1)} %param.31) | copy-start | bytes 6148
  4.8 17.0 %copy-start.12 = (bf16[2,2,1024]{2,1,0:T(2,128)(2,1)S(1)}, bf16[2,2,1024]{2,1,0:T(2,128)(2,1)}, u32[]{:S(2)}) copy-start(bf16[2,2,1024]{2,1,0:T(2,128)(2,1)} %param.29) | copy-start | bytes 24580
  4.8 17.0 %copy-start.10 = (s32[2,64,64]{2,1,0:T(8,128)S(1)}, s32[2,64,64]{2,1,0:T(8,128)}, u32[]{:S(2)}) copy-start(s32[2,64,64]{2,1,0:T(8,128)} %param.19) | copy-start | bytes 98308
  4.8 17.1 %copy-start.11 = (s32[132,2]{0,1:T(2,128)S(1)}, s32[132,2]{0,1:T(2,128)}, u32[]{:S(2)}) copy-start(s32[132,2]{0,1:T(2,128)} %param.33) | copy-start | bytes 3172
  5.1 18.2 %copy-start.6 = (bf16[2,128,512]{2,1,0:T(8,128)(2,1)S(1)}, bf16[2,128,512]{2,1,0:T(8,128)(2,1)}, u32[]{:S(2)}) copy-start(bf16[2,128,512]{2,1,0:T(8,128)(2,1)} %param.20) | copy-start | bytes 786436
  5.2 18.4 %copy-start.7 = (bf16[2,128,512]{2,1,0:T(8,128)(2,1)S(1)}, bf16[2,128,512]{2,1,0:T(8,128)(2,1)}, u32[]{:S(2)}) copy-start(bf16[2,128,512]{2,1,0:T(8,128)(2,1)} %param.21) | copy-start | bytes 786436
  5.4 18.3 %copy-start.4 = (bf16[2,64,3,512]{3,1,2,0:T(8,128)(2,1)S(1)}, bf16[2,64,3,512]{3,1,2,0:T(8,128)(2,1)}, u32[]{:S(2)}) copy-start(bf16[2,64,3,512]{3,1,2,0:T(8,128)(2,1)} %param.18) | copy-start | bytes 1179652
  6.4 73.0 %all-to-all-start = ((f32[32,2,2,528]{3,2,1,0:T(2,128)}), f32[32,2,2,528]{3,2,1,0:T(2,128)S(1)}, u32[]{:S(2)}, u32[]{:S(2)}) async-start(f32[32,2,2,528]{3,2,1,0:T(2,128)} %copy.218), calls=%async_computation | async-start | bytes 655360 | tf_op jit(solution)/shard_map/all_to_all | solution.py:271
  25.8 2.7 %copy-start.9 = (bf16[1,44,1024]{2,1,0:T(8,128)(2,1)S(1)}, bf16[1,44,1024]{2,1,0:T(8,128)(2,1)}, u32[]{:S(2)}) copy-start(bf16[1,44,1024]{2,1,0:T(8,128)(2,1)} %param.35) | copy-start | bytes 270340
  26.7 53.7 %copy-start.5 = (bf16[128,1024]{1,0:T(8,128)(2,1)S(1)}, bf16[128,1024]{1,0:T(8,128)(2,1)}, u32[]{:S(2)}) copy-start(bf16[128,1024]{1,0:T(8,128)(2,1)} %param.23) | copy-start | bytes 786436
  79.0 1.4 copy-start.1
  81.6 10.7 %copy-start.8 = (bf16[1,44,2,1024]{3,2,1,0:T(2,128)(2,1)S(1)}, bf16[1,44,2,1024]{3,2,1,0:T(2,128)(2,1)}, u32[]{:S(2)}) copy-start(bf16[1,44,2,1024]{3,2,1,0:T(2,128)(2,1)} %param.34) | copy-start | bytes 540676
  83.2 100.4 %all-to-all-start.1 = ((bf16[16,21,1024]{2,1,0:T(8,128)(2,1)}), bf16[16,21,1024]{2,1,0:T(8,128)(2,1)S(1)}, u32[]{:S(2)}, u32[]{:S(2)}) async-start(bf16[16,21,1024]{2,1,0:T(8,128)(2,1)} %reshape.241), calls=%async_computation.1 | async-start | bytes 1572864 | tf_op jit(solution)/shard_map/all_to_all | solution.py:418
  194.3 6.2 %copy-start.14 = (s32[2,8]{1,0:T(2,128)S(1)}, s32[2,8]{1,0:T(2,128)}, u32[]{:S(2)}) copy-start(s32[2,8]{1,0:T(2,128)} %param.24) | copy-start | bytes 196
  195.4 52.8 %all-to-all-start.2 = ((bf16[16,21,1024]{2,1,0:T(8,128)(2,1)}), bf16[16,21,1024]{2,1,0:T(8,128)(2,1)S(1)}, u32[]{:S(2)}, u32[]{:S(2)}) async-start(bf16[16,21,1024]{2,1,0:T(8,128)(2,1)} %reshape.246), calls=%async_computation.2 | async-start | bytes 1572864 | tf_op jit(solution)/shard_map/all_to_all | solution.py:426
  249.0 2.0 copy-start.2

commit v4 on v3

--- a/solution.py
+++ b/solution.py
@@ -93,10 +93,10 @@
     pl.semaphore_wait(barrier, neighbours)
 
     def send(k, slot, source, sem, device):
-        return lambda: remote(source(), outputs[k].at[slot], sem, recv_sem.at[k, slot], device)
+        return lambda: remote(source(), outputs[k].at[:, slot], sem, recv_sem.at[k, slot], device)
 
     def arrive(k, slot):
-        piece = outputs[k].at[slot]
+        piece = outputs[k].at[:, slot]
         remote(piece, piece, far_sem.at[k, 0], recv_sem.at[k, slot], right).wait_recv()
 
     def row_send(index, slot, source, device):
@@ -122,7 +122,7 @@
         sends_of(has_down, send(k, blk, own, down_sem.at[k, 0], below), started)
         sends_of(always, send(k, blk, own, right_sem.at[k, 0], right), started)
         sends_of(always, send(k, blk, own, left_sem.at[k, 0], left), started)
-        copy = pltpu.make_async_copy(inputs[k], outputs[k].at[blk], local_sem.at[k])
+        copy = pltpu.make_async_copy(inputs[k], outputs[k].at[:, blk], local_sem.at[k])
         copy.start()
         own_copies.append(copy)
 
@@ -144,8 +144,8 @@
                     arrive(k, from_right)
 
                 sem = far_sem.at[k, distance + direction * LINE]
-                first = lambda k=k, slot=from_left: outputs[k].at[slot]
-                second = lambda k=k, slot=from_right: outputs[k].at[slot]
+                first = lambda k=k, slot=from_left: outputs[k].at[:, slot]
+                second = lambda k=k, slot=from_right: outputs[k].at[:, slot]
                 sends_of(
                     jnp.logical_and(present, even),
                     send(k, from_left, first, sem, right),
@@ -166,7 +166,7 @@
             z_sem = up_sem if direction == 0 else down_sem
             index = distance + direction * LINE
             for k in range(count):
-                held = lambda k=k, slot=slot: outputs[k].at[slot]
+                held = lambda k=k, slot=slot: outputs[k].at[:, slot]
 
                 @pl.when(present)
                 def _(k=k, slot=slot):
@@ -230,10 +230,10 @@
 def gather_blocks(blocks, rows, collective_id):
     count = len(blocks)
     with_rows = rows is not None
-    blocks = [jnp.pad(block, ((0, SLOT - block.shape[0]), (0, 0))) for block in blocks]
-    width = blocks[0].shape[1]
+    blocks = [jnp.pad(block, ((0, 0), (0, SLOT - block.shape[1]), (0, 0))) for block in blocks]
+    layers, _, width = blocks[0].shape
     dma = pltpu.SemaphoreType.DMA
-    shapes = [jax.ShapeDtypeStruct((RING * LINE, SLOT, width), jnp.bfloat16)] * count
+    shapes = [jax.ShapeDtypeStruct((layers, RING * LINE, SLOT, width), jnp.bfloat16)] * count
     operands = list(blocks)
     scratch = [
         dma((count,)),
@@ -256,10 +256,13 @@
         scratch_shapes=scratch,
         compiler_params=pltpu.CompilerParams(collective_id=collective_id, has_side_effects=True),
         cost_estimate=pl.CostEstimate(
-            flops=0, bytes_accessed=100_000_000 * count, transcendentals=0
+            flops=0, bytes_accessed=100_000_000 * layers, transcendentals=0
         ),
     )(*operands)
-    return [array.reshape(-1, array.shape[-1]) for array in gathered]
+    weights = gathered[0].reshape(layers, -1, width)
+    if with_rows:
+        return weights, gathered[1].reshape(-1, rows.shape[-1])
+    return weights
 
 
 def scatter_parts(part, share_rows):
@@ -372,7 +375,7 @@
     local_part = block_part(long_queries, heads_of(long_keys), heads_of(long_values), everything)
     share_rows = tree_size // lax.axis_size("blk")
     share_start = lax.axis_index("blk") * share_rows
-    down_weight, projection = gather_blocks([expert_out[0]], out_weight, 0)
+    down_weight, projection = gather_blocks([expert_out], out_weight, 0)
     cache_part = join_many(scatter_parts(local_part, share_rows))
     share_queries = lax.dynamic_slice_in_dim(long_queries, share_start, share_rows, 1)
     share_mask = lax.dynamic_slice_in_dim(long_mask, share_start, share_rows, 1)
@@ -417,11 +420,11 @@
     dispatch = dispatch.reshape(expert_count, capacity, model_width)
     received = lax.all_to_all(dispatch, "expert", split_axis=0, concat_axis=0, tiled=True)
     flat_rows = received.reshape(-1, model_width)
-    gate_weight, up_weight = gather_blocks([own_in[0, :, 0, :], own_in[0, :, 1, :]], None, 1)
+    gate_weight, up_weight = gather_blocks([own_in[0].transpose(1, 0, 2)], None, 1)
     gate_part = jnp.einsum("rd,nd->rn", flat_rows, gate_weight, preferred_element_type=jnp.float32)
     up_part = jnp.einsum("rd,nd->rn", flat_rows, up_weight, preferred_element_type=jnp.float32)
     inner_act = (jax.nn.gelu(gate_part, approximate=True) * up_part).astype(jnp.bfloat16)
-    expert_sum = jnp.dot(inner_act, down_weight, preferred_element_type=jnp.float32)
+    expert_sum = jnp.dot(inner_act, down_weight[0], preferred_element_type=jnp.float32)
     expert_y = expert_sum.astype(jnp.bfloat16).reshape(expert_count, capacity, model_width)
     returned = lax.all_to_all(expert_y, "expert", split_axis=0, concat_axis=0, tiled=True)
     per_route = jnp.einsum(

time: 252 us -> 260 us (1.032)
  local copies, waits for them, and re-layouts: 14.1 us -> 20.2 us
    another operation x0 -> x1, local copies, waits for them, and re-layouts: none -> 6.73 us  [on_device(): gate_weight, up_weight = gather_blocks([own_in[0].transpose(1, 0, 2)], No...]
  transfers between devices with their start and end apart: 3 -> 3, of which waited for: 1 -> 1; matrix products, arithmetic and copies ran while one was open for 4% -> 6% of each run, Pallas kernels for 56% -> 54%
where the time goes in v4:
time: 260 us
  Pallas kernels  141 us (54%)
  waiting for transfers between devices  47.1 us (18%)
  starting transfers between devices  30.1 us (12%)
  local copies, waits for them, and re-layouts  20.2 us (8%)
  matrix products  14.7 us (6%)
  other arithmetic  4.65 us (2%)
    pallas_call x2, Pallas kernels, gather_blocks(): pl.pallas_call(functools.partial(gather_kernel, count, with_rows), out_sh...  141 us
    all_to_all x1, waiting for transfers between devices, on_device(): lax.all_to_all(expert_y, 'expert', split_axis=0, concat_axis=0, tiled=True)  47.1 us
    all_to_all x1, starting transfers between devices, scatter_parts(): lax.all_to_all(packed, 'blk', split_axis=0, concat_axis=0, tiled=True)  15.2 us
    all_to_all x1, starting transfers between devices, on_device(): lax.all_to_all(dispatch, 'expert', split_axis=0, concat_axis=0, tiled=True)  9.08 us
    another operation x1, local copies, waits for them, and re-layouts, on_device(): gate_weight, up_weight = gather_blocks([own_in[0].transpose(1, 0, 2)], No...  6.73 us
    dot_general x1, matrix products, on_device(): jnp.dot(inner_act, down_weight[0], preferred_element_type=jnp.float32)  5.91 us
    all_to_all x1, starting transfers between devices, on_device(): lax.all_to_all(expert_y, 'expert', split_axis=0, concat_axis=0, tiled=True)  5.75 us
  transfers between devices with their start and end apart: 3, of which 1 were waited for; matrix products, arithmetic and copies ran while one was open for 6% of the time, Pallas kernels for 54%

profile of v4, /device:TPU:32, one launch (start us, length us, event | category | flops | bytes accessed | tf_op | source)
XLA Modules:
  0.0 259.6 jit_solution(16627000321237765166)
XLA Ops:
  0.6 1.1 fusion.63
  1.7 0.2 reshape_squeeze.21
  1.9 1.3 copy.206
  3.2 0.4 fusion.65
  3.7 0.4 convert_reduce_fusion
  4.2 0.2 copy.208
  4.4 0.4 convolution_bitcast_fusion.2
  4.8 0.3 copy.209
  5.2 0.2 concatenate.17
  5.4 0.2 maximum_bitcast_fusion
  5.6 0.8 copy.212
  6.4 15.2 %all-to-all-start = ((f32[32,2,2,528]{3,2,1,0:T(2,128)}), f32[32,2,2,528]{3,2,1,0:T(2,128)S(1)}, u32[]{:S(2)}, u32[]{:S(2)}) async-start(f32[32,2,2,528]{3,2,1,0:T(2,128)} %copy.212), calls=%async_computation | async-start | bytes 655360 | tf_op jit(solution)/shard_map/all_to_all | solution.py:274
  22.1 0.1 reshape.233
  22.2 0.9 reduce-window.6
  23.1 0.2 slice_reduce_fusion.1
  23.4 0.2 copy.197
  23.6 0.2 copy.199
  23.8 0.2 reshape_squeeze.18
  24.0 0.2 reshape_squeeze.20
  24.2 0.2 reshape_squeeze.19
  24.4 0.3 fusion.66
  24.6 0.4 fusion.67
  25.0 0.4 convert_reduce_fusion.2
  25.4 0.1 convert_reduce_fusion.1
  25.5 0.3 fusion.13
  25.9 0.5 fusion.20
  26.4 0.2 copy.205
  26.6 0.2 convert_element_type.80
  26.8 0.2 reshape_squeeze.23
  27.0 0.2 reshape_squeeze.22
  27.2 0.7 dynamic-slice_compare_fusion
  27.9 0.3 fusion.64
  28.3 0.2 convert_reduce_fusion.3
  28.6 0.7 pad.12.refs_0_
  29.2 49.8 %shard_map.193 = (bf16[1,32,48,1024]{3,2,1,0:T(8,128)(2,1)}, bf16[16,32,1024]{2,1,0:T(8,128)(2,1)}) custom-call(bf16[1,48,1024]{2,1,0:T(8,128)(2,1)} %pad.12.refs_0_, bf16[32,1024]{1,0:T(8,128)(2,1)} %refs_1_.1), custom_call_target="tpu_custom_call" | custom-call | bytes 100000000 | tf_op jit(solution)/shard_map/pallas_call | solution.py:251
  79.2 0.2 fusion.28
  79.5 0.1 fusion.39
  79.6 0.2 mul.189
  79.8 0.2 mul.190
  80.1 0.2 fusion.27
  80.5 0.4 multiply_reduce_fusion
  80.9 0.1 multiply_convert_fusion
  81.1 0.3 broadcast_in_dim.98
  81.4 0.2 reshape.236
  81.6 0.5 convolution_convert_fusion.1
  82.1 1.1 reshape.237
  83.3 9.1 %all-to-all-start.1 = ((bf16[16,21,1024]{2,1,0:T(8,128)(2,1)}), bf16[16,21,1024]{2,1,0:T(8,128)(2,1)S(1)}, u32[]{:S(2)}, u32[]{:S(2)}) async-start(bf16[16,21,1024]{2,1,0:T(8,128)(2,1)} %reshape.237), calls=%async_computation.1 | async-start | bytes 1572864 | tf_op jit(solution)/shard_map/all_to_all | solution.py:421
  92.4 0.7 pad.14.refs_0_
  93.1 91.6 %shard_map.194 = bf16[2,32,48,1024]{3,2,1,0:T(8,128)(2,1)} custom-call(bf16[2,48,1024]{2,1,0:T(8,128)(2,1)} %pad.14.refs_0_), custom_call_target="tpu_custom_call" | custom-call | bytes 200000000 | tf_op jit(solution)/shard_map/pallas_call | solution.py:251
  184.7 6.7 %fusion.61 = (bf16[1,32,48,1024]{3,2,1,0:T(8,128)(2,1)}, bf16[1,32,48,1024]{3,2,1,0:T(8,128)(2,1)}) fusion(bf16[2,32,48,1024]{3,2,1,0:T(8,128)(2,1)} %shard_map.194), kind=kLoop, calls=%fused_computation.117 | loop fusion | bytes 12582912 | tf_op jit(solution)/shard_map/unstack | solution.py:423
  191.5 0.2 reshape.238
  191.7 4.5 %fusion.68 = f32[336,1536]{1,0:T(8,128)} fusion(bf16[336,1024]{1,0:T(8,128)(2,1)S(1)} %reshape.238, bf16[1536,1024]{1,0:T(8,128)(2,1)} %bitcast.118), kind=kOutput, calls=%fused_computation.124 | convolution fusion | flops 1056964608 | bytes 5898240 | tf_op jit(solution)/shard_map/rd,nd->rn/dot_general | solution.py:424
  196.2 5.9 %convolution_convert_fusion = bf16[336,1024]{1,0:T(8,128)(2,1)S(1)} fusion(bf16[1536,1024]{1,0:T(8,128)(2,1)} %bitcast.129, bf16[336,1024]{1,0:T(8,128)(2,1)S(1)} %reshape.238, bf16[1536,1024]{1,0:T(8,128)(2,1)} %bitcast.117, f32[336,1536]{1,0:T(8,128)} %fusion.68), kind=kOutput, calls=%fused_computation.14 | convolution fusion | flops 2119434240 | bytes 9732096 | tf_op jit(solution)/shard_map/dot_general | solution.py:427
  202.1 1.1 reshape.239
  203.2 5.8 %all-to-all-start.2 = ((bf16[16,21,1024]{2,1,0:T(8,128)(2,1)}), bf16[16,21,1024]{2,1,0:T(8,128)(2,1)S(1)}, u32[]{:S(2)}, u32[]{:S(2)}) async-start(bf16[16,21,1024]{2,1,0:T(8,128)(2,1)} %reshape.239), calls=%async_computation.2 | async-start | bytes 1572864 | tf_op jit(solution)/shard_map/all_to_all | solution.py:429
  209.1 0.1 iota_compare_fusion.2
  209.2 0.1 eq.80
  209.4 0.2 fusion.23
  209.6 47.1 %all-to-all-done.2 = bf16[16,21,1024]{2,1,0:T(8,128)(2,1)S(1)} async-done(((bf16[16,21,1024]{2,1,0:T(8,128)(2,1)}), bf16[16,21,1024]{2,1,0:T(8,128)(2,1)S(1)}, u32[]{:S(2)}, u32[]{:S(2)}) %all-to-all-start.2) | async-done | bytes 688160 | tf_op jit(solution)/shard_map/all_to_all | solution.py:429
  256.7 0.2 reshape.255
  256.9 0.5 fusion.9
  257.5 0.7 reshape.242
  258.2 0.7 gather_fusion
  258.9 0.7 bitcast_select_fusion
  (67 shorter events, 1.6 us)
Async XLA Ops:
  0.6 208.8 %copy-start = (bf16[1024,16]{0,1:T(8,128)(2,1)S(1)}, bf16[1024,16]{0,1:T(8,128)(2,1)}, u32[]{:S(2)}) copy-start(bf16[1024,16]{0,1:T(8,128)(2,1)} %param.32) | copy-start | bytes 98308
  1.9 2.3 copy-start.3
  4.8 16.9 %copy-start.15 = (s32[2]{0:T(128)S(1)}, s32[2]{0:T(128)}, u32[]{:S(2)}) copy-start(s32[2]{0:T(128)} %param.22) | copy-start | bytes 28
  4.8 17.0 %copy-start.13 = (bf16[1024]{0:T(1024)(128)(2,1)S(1)}, bf16[1024]{0:T(1024)(128)(2,1)}, u32[]{:S(2)}) copy-start(bf16[1024]{0:T(1024)(128)(2,1)} %param.31) | copy-start | bytes 6148
  4.8 17.0 %copy-start.12 = (bf16[2,2,1024]{2,1,0:T(2,128)(2,1)S(1)}, bf16[2,2,1024]{2,1,0:T(2,128)(2,1)}, u32[]{:S(2)}) copy-start(bf16[2,2,1024]{2,1,0:T(2,128)(2,1)} %param.29) | copy-start | bytes 24580
  4.8 17.0 %copy-start.10 = (s32[2,64,64]{2,1,0:T(8,128)S(1)}, s32[2,64,64]{2,1,0:T(8,128)}, u32[]{:S(2)}) copy-start(s32[2,64,64]{2,1,0:T(8,128)} %param.19) | copy-start | bytes 98308
  4.8 17.1 %copy-start.11 = (s32[132,2]{0,1:T(2,128)S(1)}, s32[132,2]{0,1:T(2,128)}, u32[]{:S(2)}) copy-start(s32[132,2]{0,1:T(2,128)} %param.33) | copy-start | bytes 3172
  5.2 18.2 %copy-start.6 = (bf16[2,128,512]{2,1,0:T(8,128)(2,1)S(1)}, bf16[2,128,512]{2,1,0:T(8,128)(2,1)}, u32[]{:S(2)}) copy-start(bf16[2,128,512]{2,1,0:T(8,128)(2,1)} %param.20) | copy-start | bytes 786436
  5.2 18.4 %copy-start.7 = (bf16[2,128,512]{2,1,0:T(8,128)(2,1)S(1)}, bf16[2,128,512]{2,1,0:T(8,128)(2,1)}, u32[]{:S(2)}) copy-start(bf16[2,128,512]{2,1,0:T(8,128)(2,1)} %param.21) | copy-start | bytes 786436
  5.4 18.4 %copy-start.4 = (bf16[2,64,3,512]{3,1,2,0:T(8,128)(2,1)S(1)}, bf16[2,64,3,512]{3,1,2,0:T(8,128)(2,1)}, u32[]{:S(2)}) copy-start(bf16[2,64,3,512]{3,1,2,0:T(8,128)(2,1)} %param.18) | copy-start | bytes 1179652
  6.4 73.0 %all-to-all-start = ((f32[32,2,2,528]{3,2,1,0:T(2,128)}), f32[32,2,2,528]{3,2,1,0:T(2,128)S(1)}, u32[]{:S(2)}, u32[]{:S(2)}) async-start(f32[32,2,2,528]{3,2,1,0:T(2,128)} %copy.212), calls=%async_computation | async-start | bytes 655360 | tf_op jit(solution)/shard_map/all_to_all | solution.py:274
  25.9 2.7 %copy-start.9 = (bf16[1,44,1024]{2,1,0:T(8,128)(2,1)S(1)}, bf16[1,44,1024]{2,1,0:T(8,128)(2,1)}, u32[]{:S(2)}) copy-start(bf16[1,44,1024]{2,1,0:T(8,128)(2,1)} %param.35) | copy-start | bytes 270340
  26.8 53.7 %copy-start.5 = (bf16[128,1024]{1,0:T(8,128)(2,1)S(1)}, bf16[128,1024]{1,0:T(8,128)(2,1)}, u32[]{:S(2)}) copy-start(bf16[128,1024]{1,0:T(8,128)(2,1)} %param.23) | copy-start | bytes 786436
  79.1 1.4 copy-start.1
  81.6 10.8 %copy-start.8 = (bf16[1,44,2,1024]{3,2,1,0:T(2,128)(2,1)S(1)}, bf16[1,44,2,1024]{3,2,1,0:T(2,128)(2,1)}, u32[]{:S(2)}) copy-start(bf16[1,44,2,1024]{3,2,1,0:T(2,128)(2,1)} %param.34) | copy-start | bytes 540676
  83.3 108.2 %all-to-all-start.1 = ((bf16[16,21,1024]{2,1,0:T(8,128)(2,1)}), bf16[16,21,1024]{2,1,0:T(8,128)(2,1)S(1)}, u32[]{:S(2)}, u32[]{:S(2)}) async-start(bf16[16,21,1024]{2,1,0:T(8,128)(2,1)} %reshape.237), calls=%async_computation.1 | async-start | bytes 1572864 | tf_op jit(solution)/shard_map/all_to_all | solution.py:421
  202.1 6.9 %copy-start.14 = (s32[2,8]{1,0:T(2,128)S(1)}, s32[2,8]{1,0:T(2,128)}, u32[]{:S(2)}) copy-start(s32[2,8]{1,0:T(2,128)} %param.24) | copy-start | bytes 196
  203.2 53.5 %all-to-all-start.2 = ((bf16[16,21,1024]{2,1,0:T(8,128)(2,1)}), bf16[16,21,1024]{2,1,0:T(8,128)(2,1)S(1)}, u32[]{:S(2)}, u32[]{:S(2)}) async-start(bf16[16,21,1024]{2,1,0:T(8,128)(2,1)} %reshape.239), calls=%async_computation.2 | async-start | bytes 1572864 | tf_op jit(solution)/shard_map/all_to_all | solution.py:429
  257.5 2.0 copy-start.2
